TPU v7x, 256 devices: a whole 4x4x8 slice. The times are simulated.
256 devices in a mesh: freq: 16 (over y_lo, x, core), row: 16 (over y_hi, z).
Axes of the slice: x: 4, y: 4 (y_hi: 2, y_lo: 2; y = y_hi * 2 + y_lo), z: 8, core: 2. Of those that a mesh axis runs over, the one named last changes fastest.
Arguments:
- source: bfloat16 [16, 2, 256, 512], P('freq', None, 'row'), may hold values from -6 to 6
- receiver: bfloat16 [16, 2, 256, 512], P('freq', None, 'row'), may hold values from -6 to 6
- filters: bfloat16 [16, 2, 2, 25, 25], P('freq'), may hold values from -0.15625 to 0.15625
- table_index: int32 [2, 256, 512], P(None, 'row'), may hold values from 0 to 1
- lags: int32 [16], replicated, may hold values from 0 to 15, each once
- offset_filters: float32 [16, 9, 9], P('freq'), may hold values from -0.125 to 0.125
Outputs:
- image: float32 [2, 16, 256, 512], P(None, 'freq', 'row')
Inputs may be any that keep to these rules, and one draw needn't show every extreme that they name: `lags`: each of 0 .. 15 appears exactly once.
All inputs are finite; a program needn't handle non-finite values.
Results may differ from a plain program's by a relative error of at most 0.0052.
Values may be sent and summed in bfloat16 or wider, within the bound.
No kernel may reach another device: no remote copies, remote signals or barrier semaphores. Data moves between devices by JAX's collectives and lax.ppermute only.
A program may use at most 128 MiB of HBM per device.

v0:
```python
import jax
import jax.numpy as jnp
from jax import lax
from jax.sharding import PartitionSpec as P

NV = 2
FILT = 25
COLBLK = 128
NOFF = 16
OFILT = 9
DEPTHS = 2


def padded_2(cells, sides, width):
    for axis, dim in sides:
        count = lax.axis_size(axis)
        ends = count - 1
        head = lax.slice_in_dim(cells, 0, width, axis=dim)
        tail = lax.slice_in_dim(cells, cells.shape[dim] - width, cells.shape[dim], axis=dim)
        cells = jnp.concatenate(
            [
                lax.ppermute(tail, axis, [(i, (i + 1) % count) for i in range(ends)]),
                cells,
                lax.ppermute(head, axis, [((i + 1) % count, i) for i in range(ends)]),
            ],
            axis=dim,
        )
    return cells


def filter_matrix(filters):
    half = (FILT - 1) // 2
    window = COLBLK + 2 * half
    real_part = filters[:, :, 0]
    imag_part = filters[:, :, 1]
    plain = jnp.stack(
        [jnp.stack([real_part, -imag_part], 2), jnp.stack([imag_part, real_part], 2)], 2
    )
    conjugate = jnp.stack(
        [jnp.stack([real_part, imag_part], 2), jnp.stack([-imag_part, real_part], 2)], 2
    )
    both = jnp.stack([plain, conjugate])
    tap_ids = lax.broadcasted_iota(jnp.int32, (FILT, window, COLBLK), 0)
    win_ids = lax.broadcasted_iota(jnp.int32, (FILT, window, COLBLK), 1)
    col_ids = lax.broadcasted_iota(jnp.int32, (FILT, window, COLBLK), 2)
    band = (win_ids - col_ids == tap_ids).astype(jnp.bfloat16)
    matrix = jnp.einsum("gfvocab,bwj->gfacwvoj", both, band, preferred_element_type=jnp.float32)
    return matrix.astype(jnp.bfloat16)


def extrapolate(fields, matrix, index):
    half = (FILT - 1) // 2
    rows = fields.shape[3]
    width = fields.shape[4]
    nblocks = width // COLBLK
    padded = padded_2(fields, (("row", 3),), half)
    padded = jnp.pad(padded, ((0, 0), (0, 0), (0, 0), (0, 0), (half, COLBLK - half)))
    blocks = padded.reshape(padded.shape[:4] + (nblocks + 1, COLBLK))
    windows = jnp.concatenate([blocks[..., :nblocks, :], blocks[..., 1:, : 2 * half]], axis=-1)
    output = None
    for tap in range(FILT):
        layer = windows[:, :, :, tap : tap + rows]
        term = jnp.einsum(
            "gfcrnw,gfcwvoj->gfovrnj", layer, matrix[:, :, tap], preferred_element_type=jnp.float32
        )
        output = term if output is None else output + term
    classes = lax.broadcasted_iota(jnp.int32, (NV, 1, 1, 1), 0)
    hot = (index.reshape((1, rows, nblocks, COLBLK)) == classes).astype(jnp.float32)
    chosen = jnp.sum(output * hot[None, None, None], axis=3)
    chosen = chosen.reshape(chosen.shape[:4] + (width,))
    return chosen.astype(jnp.bfloat16)


def correlate(fields, chosen_lags):
    shift = NOFF // 2
    width = fields.shape[4]
    padded = jnp.pad(fields, ((0, 0), (0, 0), (0, 0), (0, 0), (shift, shift)))

    def one_lag(lag):
        offset = lag - shift
        down = lax.dynamic_slice_in_dim(padded[0], shift - offset, width, 3)
        up = lax.dynamic_slice_in_dim(padded[1], shift + offset, width, 3)
        return jnp.sum(down.astype(jnp.float32) * up.astype(jnp.float32), axis=(0, 1))

    return lax.map(one_lag, chosen_lags)


def body(source, receiver, filters, table_index, lags, offset_filters):
    ohalf = (OFILT - 1) // 2
    matrix = filter_matrix(filters)
    fields = jnp.stack([source, receiver])
    owned = lags.shape[0] // lax.axis_size("freq")
    images = []
    for depth in range(DEPTHS):
        fields = extrapolate(fields, matrix, table_index[depth])

        def term(start, count):
            return correlate(fields, lags)

        images.append(
            lax.psum_scatter(
                term(jnp.int32(0), owned * lax.axis_size("freq")),
                "freq",
                scatter_dimension=0,
                tiled=True,
            )
        )
    raw = jnp.stack(images)
    padded = padded_2(raw, (("row", 2),), ohalf)
    padded = jnp.pad(padded, ((0, 0), (0, 0), (0, 0), (ohalf, ohalf)))
    kernel = offset_filters[:, None]
    return lax.conv_general_dilated(
        padded,
        kernel,
        (1, 1),
        ((0, 0), (0, 0)),
        dimension_numbers=("NCHW", "OIHW", "NCHW"),
        feature_group_count=offset_filters.shape[0],
        precision=lax.Precision.HIGHEST,
    )


def solution(mesh):
    in_specs = (
        P("freq", None, "row", None),
        P("freq", None, "row", None),
        P("freq", None, None, None, None),
        P(None, "row", None),
        P(),
        P("freq", None, None),
    )
    out_specs = P(None, "freq", "row", None)
    return jax.shard_map(body, mesh=mesh, in_specs=in_specs, out_specs=out_specs, check_vma=False)
```

profile of v0, /device:TPU:224, one launch (start us, length us, event | category | flops | bytes accessed | tf_op | source)
XLA Modules:
  0.0 425.4 jit_solution(18421759945478041566)
XLA Ops:
  6.5 0.9 slice_maximum_fusion
  7.4 1.9 collective-permute-start
  9.3 3.9 collective-permute-start.1
  13.3 0.8 copy.755
  14.1 9.4 %convert_bitcast_fusion = bf16[2,1,25,2,152,2,2,128]{7,2,3,6,5,0,4,1:T(8,128)(2,1)} fusion(bf16[1,1,2,2,2,25,25]{6,5,4,3,2,0,1:T(8,128)(2,1)S(1)} %maximum_bitcast_fusion.4, bf16[1,2,1,2,25,25]{5,4,3,1,2,0:T(8,128)(2,1)S(1)} %get-tuple-element.279, bf16[1,2,1,2,25,25]{5,4,3,1,2,0:T(8,128)(2,1)S(1)} %get-tuple-element.272), kind=kOutput, calls=%fused_computation.4 | convolution fusion | flops 397920192 | bytes 15584800 | tf_op jit(solution)/shard_map/gfvocab,bwj->gfacwvoj/dot_general | solution.py:47
  23.5 17.2 %fusion.179 = (bf16[2,1,1,2,152,2,2,128]{7,2,3,6,5,0,4,1:T(2,128)(2,1)}, bf16[2,1,1,2,152,2,2,128]{7,2,3,6,5,0,4,1:T(2,128)(2,1)}, bf16[2,1,1,2,152,2,2,128]{7,2...) fusion(bf16[2,1,25,2,152,2,2,128]{7,2,3,6,5,0,4,1:T(8,128)(2,1), ...), kind=kLoop, calls=%fused_computation.315 | loop fusion | bytes 7471104 | tf_op jit(solution)/shard_map/slice | solution.py:64
  40.8 44.9 %fusion.178 = (bf16[2,1,1,2,152,2,2,128]{7,2,3,6,5,0,4,1:T(2,128)(2,1)}, bf16[2,1,1,2,152,2,2,128]{7,2,3,6,5,0,4,1:T(2,128)(2,1)}, bf16[2,1,1,2,152,2,2,128]{7,2...) fusion(bf16[2,1,25,2,152,2,2,128]{7,2,3,6,5,0,4,1:T(8,128)(2,1), ...), kind=kLoop, calls=%fused_computation.314 | loop fusion | bytes 23658496 | tf_op jit(solution)/shard_map/slice | solution.py:64
  86.5 1.0 copy-done.26
  98.1 0.7 copy-done
  104.7 5.5 %collective-permute-start.2 = (bf16[2,1,2,12,512]{4,3,2,0,1:T(8,128)(2,1)S(1)}, bf16[2,1,2,12,512]{4,3,2,0,1:T(8,128)(2,1)S(1)}, u32[]{:S(2)}, u32[]{:S(2)}) collective-permute-start(bf16[2,1,2,12,512]{4,3,2,0,1:T(8,128)(2,1)S(1)} %get-tuple-element.268), channel_id=1, source_target_pairs={{0,1},{1,2},{2,3},{3,4},{4,5},{5,6},{6,7},{7,8},{8,9},{9,10},{10,1... | collective-permute-start | bytes 147464 | tf_op jit(solution)/shard_map/ppermute | solution.py:22
  110.2 1.9 collective-permute-start.3
  112.2 46.7 %while.30 = (s32[]{:T(128)}, f32[16,16,512]{2,1,0:T(8,128)S(1)}, bf16[2,1,2,16,528]{4,3,2,1,0:T(8,128)(2,1)S(1)}, s32[16]{0:T(128)S(1)}, s32[]{:T(128)}, /*index...) while((s32[]{:T(128)}, f32[16,16,512]{2,1,0:T(8,128)S(1)}, ...), condition=%wide.region_3.4_spmd, body=%wide.region_1.3_spmd.sunk | while | flops 57354 | bytes 299233 | solution.py:85
  158.9 0.8 copy-done.4
  160.7 1.0 copy-done.47
  172.5 0.7 copy-done.1
  179.1 53.3 %while.31 = (s32[]{:T(128)}, f32[16,16,512]{2,1,0:T(8,128)S(1)}, bf16[2,1,2,16,528]{4,3,2,1,0:T(8,128)(2,1)S(1)}, s32[16]{0:T(128)S(1)}, s32[]{:T(128)}, /*index...) while((s32[]{:T(128)}, f32[16,16,512]{2,1,0:T(8,128)S(1)}, ...), condition=%wide.region_8.9_spmd, body=%wide.region_6.8_spmd.sunk | while | flops 57354 | bytes 299233 | solution.py:85
  179.1 0.6 dynamic_slice.48
  182.5 0.6 dynamic_slice.48
  185.8 0.6 dynamic_slice.48
  192.5 0.6 dynamic_slice.48
  195.8 0.6 dynamic_slice.48
  199.1 0.6 dynamic_slice.48
  232.4 0.8 copy-done.5
  233.2 65.3 %reduce-scatter.5.cloned.1.call-done = f32[1,16,512]{2,1,0:T(8,128)} async-done(((f32[16,16,512]{2,1,0:T(8,128)}), f32[1,16,512]{2,1,0:T(8,128)}) %reduce-scatter.5.cloned.1.call-update) | async-done | bytes 32784 | tf_op jit(solution)/shard_map/reduce_scatter | solution.py:101
  298.6 0.8 pad_maximum_fusion.4
  299.3 4.0 collective-permute-start.4
  303.3 2.1 collective-permute-start.5
  305.6 6.9 %collective-permute-done.5 = f32[2,1,4,512]{3,2,1,0:T(4,128)S(1)} collective-permute-done((f32[2,1,4,512]{3,2,1,0:T(4,128)S(1)}, f32[2,1,4,512]{3,2,1,0:T(4,128)S(1)}, u32[]{:S(2)}, u32[]{:S(2)}) %collective-permute-start.5) | collective-permute-done | bytes 16416 | tf_op jit(solution)/shard_map/ppermute | solution.py:24
  312.6 0.8 maximum_bitcast_fusion.2
  314.0 0.6 copy.336
  314.6 102.5 %broadcast_select_fusion = f32[16,16,65,1]{1,3,2,0:T(1,128)S(1)} fusion(pred[16,65]{0,1:T(8,128)(4,1)S(1)} %copy-done.53, f32[1,24,16,73]{2,0,3,1:T(1,128)S(1)} %copy.336, f32[1,1,9,9]{1,0,3,2:T(1,128)S(1)} %copy.337), kind=kOutput, calls=%fused_computation.113 | convolution fusion | flops 16190720 | bytes 180052 | tf_op jit(solution)/shard_map/conv_general_dilated | solution.py:112
  417.7 0.6 copy.339
  (324 shorter events, 54.5 us)
Async XLA Ops:
  6.5 226.7 %reduce-scatter.3.cloned.1.call-start = ((), (), s32[]{:S(2)}) async-start(), calls=%async_computation.2 | async-start | bytes 557056 | tf_op jit(solution)/shard_map/reduce_scatter | solution.py:101
  7.4 78.4 %collective-permute-start = (bf16[2,1,2,12,512]{4,3,2,1,0:T(8,128)(2,1)S(1)}, bf16[2,1,2,12,512]{4,3,2,1,0:T(8,128)(2,1)S(1)}, u32[]{:S(2)}, u32[]{:S(2)}) collective-permute-start(bf16[2,1,2,12,512]{4,3,2,1,0:T(8,128)(2,1)S(1)} %get-tuple-element.270), channel_id=1, source_target_pairs={{0,1},{1,2},{2,3},{3,4},{4,5},{5,6},{6,7},{7,8},{8,9},{9,10},{10,1... | collective-permute-start | bytes 147464 | tf_op jit(solution)/shard_map/ppermute | solution.py:22
  9.3 76.5 %collective-permute-start.1 = (bf16[2,1,2,12,512]{4,3,2,1,0:T(8,128)(2,1)S(1)}, bf16[2,1,2,12,512]{4,3,2,1,0:T(8,128)(2,1)S(1)}, u32[]{:S(2)}, u32[]{:S(2)}) collective-permute-start(bf16[2,1,2,12,512]{4,3,2,1,0:T(8,128)(2,1)S(1)} %get-tuple-element.271), channel_id=1, source_target_pairs={{1,0},{2,1},{3,2},{4,3},{5,4},{6,5},{7,6},{8,7},{9,8},{10,9},{11,1... | collective-permute-start | bytes 147464 | tf_op jit(solution)/shard_map/ppermute | solution.py:24
  40.8 44.9 %copy-start.50 = (s32[2,16,512]{2,1,0:T(8,128)S(1)}, s32[2,16,512]{2,1,0:T(8,128)}, u32[]{:S(2)}) copy-start(s32[2,16,512]{2,1,0:T(8,128)} %param.13) | copy-start | bytes 196612
  40.8 45.0 %copy-start.48 = (bf16[1,2,16,512]{3,2,1,0:T(8,128)(2,1)S(1)}, bf16[1,2,16,512]{3,2,1,0:T(8,128)(2,1)}, u32[]{:S(2)}) copy-start(bf16[1,2,16,512]{3,2,1,0:T(8,128)(2,1)} %param.11) | copy-start | bytes 98308
  40.8 45.0 %copy-start.49 = (bf16[1,2,16,512]{3,2,1,0:T(8,128)(2,1)S(1)}, bf16[1,2,16,512]{3,2,1,0:T(8,128)(2,1)}, u32[]{:S(2)}) copy-start(bf16[1,2,16,512]{3,2,1,0:T(8,128)(2,1)} %param.10) | copy-start | bytes 98308
  86.3 1.7 copy-start.24
  87.5 1.4 copy-start.22
  88.0 1.4 copy-start.20
  88.5 1.5 copy-start.18
  89.4 1.4 copy-start.46
  90.0 1.4 copy-start.44
  90.8 1.4 copy-start.42
  91.4 1.4 copy-start.40
  93.3 1.5 copy-start.34
  94.1 1.4 copy-start.32
  94.7 1.4 copy-start.30
  99.8 1.4 copy-start.14
  103.8 8.3 %copy-start.52 = (s32[16]{0:T(128)S(1)}, s32[16]{0:T(128)}, u32[]{:S(2)}) copy-start(s32[16]{0:T(128)} %param.14) | copy-start | bytes 196
  104.7 55.3 %collective-permute-start.2 = (bf16[2,1,2,12,512]{4,3,2,0,1:T(8,128)(2,1)S(1)}, bf16[2,1,2,12,512]{4,3,2,0,1:T(8,128)(2,1)S(1)}, u32[]{:S(2)}, u32[]{:S(2)}) collective-permute-start(bf16[2,1,2,12,512]{4,3,2,0,1:T(8,128)(2,1)S(1)} %get-tuple-element.268), channel_id=1, source_target_pairs={{0,1},{1,2},{2,3},{3,4},{4,5},{5,6},{6,7},{7,8},{8,9},{9,10},{10,1... | collective-permute-start | bytes 147464 | tf_op jit(solution)/shard_map/ppermute | solution.py:22
  110.2 49.8 %collective-permute-start.3 = (bf16[2,1,2,12,512]{4,3,2,0,1:T(8,128)(2,1)S(1)}, bf16[2,1,2,12,512]{4,3,2,0,1:T(8,128)(2,1)S(1)}, u32[]{:S(2)}, u32[]{:S(2)}) collective-permute-start(bf16[2,1,2,12,512]{4,3,2,0,1:T(8,128)(2,1)S(1)} %get-tuple-element.269), channel_id=1, source_target_pairs={{1,0},{2,1},{3,2},{4,3},{5,4},{6,5},{7,6},{8,7},{9,8},{10,9},{11,1... | collective-permute-start | bytes 147464 | tf_op jit(solution)/shard_map/ppermute | solution.py:24
  159.7 138.8 %reduce-scatter.5.cloned.1.call-start = ((), (), s32[]{:S(2)}) async-start(), calls=%async_computation.3 | async-start | bytes 557056 | tf_op jit(solution)/shard_map/reduce_scatter | solution.py:101
  160.5 1.7 copy-start.45
  162.2 1.4 copy-start.41
  167.7 1.4 copy-start.25
  170.5 1.4 copy-start.3
  174.2 1.4 copy-start.15
  176.4 1.4 copy-start.9
  177.0 1.4 copy-start.7
  179.1 126.3 %copy-start.51 = (f32[1,9,9]{2,0,1:T(1,128)S(1)}, f32[1,9,9]{2,0,1:T(1,128)}, u32[]{:S(2)}) copy-start(f32[1,9,9]{2,0,1:T(1,128)} %param.15) | copy-start | bytes 976
  299.3 6.3 %collective-permute-start.4 = (f32[2,1,4,512]{3,2,1,0:T(4,128)S(1)}, f32[2,1,4,512]{3,2,1,0:T(4,128)S(1)}, u32[]{:S(2)}, u32[]{:S(2)}) collective-permute-start(f32[2,1,4,512]{3,2,1,0:T(4,128)S(1)} %get-tuple-element.264), channel_id=1, source_target_pairs={{0,1},{1,2},{2,3},{3,4},{4,5},{5,6},{6,7},{7,8},{8,9},{9,10},{10,1... | collective-permute-start | bytes 49160 | tf_op jit(solution)/shard_map/ppermute | solution.py:22
  303.3 9.2 %collective-permute-start.5 = (f32[2,1,4,512]{3,2,1,0:T(4,128)S(1)}, f32[2,1,4,512]{3,2,1,0:T(4,128)S(1)}, u32[]{:S(2)}, u32[]{:S(2)}) collective-permute-start(f32[2,1,4,512]{3,2,1,0:T(4,128)S(1)} %get-tuple-element.265), channel_id=1, source_target_pairs={{1,0},{2,1},{3,2},{4,3},{5,4},{6,5},{7,6},{8,7},{9,8},{10,9},{11,1... | collective-permute-start | bytes 49160 | tf_op jit(solution)/shard_map/ppermute | solution.py:24
  (30 other events, 39.5 us)
Sparse Core Ops, SparseCore 0:
  159.9 65.2 reduce-scatter.2
  233.3 65.1 reduce-scatter.4
where the time goes:
time: 433 us; the launch traced here: 425 us
  matrix products  137 us (32%)
  local copies, waits for them, and re-layouts  98.4 us (23%)
  loops' own time  77.4 us (18%)
  waiting for transfers between devices  72.3 us (17%)
  starting transfers between devices  19.6 us (5%)
  between operations  14.6 us (3%)
  other arithmetic  6.08 us (1%)
    conv_general_dilated x1, matrix products, body(): lax.conv_general_dilated(padded, kernel, (1, 1), ((0, 0), (0, 0)), dimens...  103 us
    another operation x2, loops' own time, correlate(): return lax.map(one_lag, chosen_lags)  77.4 us
    reduce_scatter x2, waiting for transfers between devices, body(): lax.psum_scatter(term(jnp.int32(0), owned * lax.axis_size('freq')), 'freq...  65.3 us
    slice x2, local copies, waits for them, and re-layouts, extrapolate(): matrix[:, :, tap]  62.1 us
    dot_general x50, matrix products, extrapolate(): jnp.einsum('gfcrnw,gfcwvoj->gfovrnj', layer, matrix[:, :, tap], preferred...  25 us
    dynamic_slice x32, local copies, waits for them, and re-layouts, correlate(): return lax.map(one_lag, chosen_lags)  18.8 us
    unnamed x112, local copies, waits for them, and re-layouts  13.2 us
    ppermute x3, starting transfers between devices, padded_2(): lax.ppermute(tail, axis, [(i, (i + 1) % count) for i in range(ends)])  11.4 us
  transfers between devices with their start and end apart: 8, of which 2 were waited for; matrix products, arithmetic and copies ran while one was open for 25% of the time, Pallas kernels for 0%

commit v1 on v0

v1 whole, which is shorter than its diff:
```python
import jax
import jax.numpy as jnp
from jax import lax
from jax.experimental import pallas as pl
from jax.experimental.pallas import tpu as pltpu
from jax.sharding import PartitionSpec as P

NV = 2
FILT = 25
HALF = 12
NOFF = 16
OFILT = 9
OHALF = 4
DEPTHS = 2
ROWS = 16
WIDTH = 512
BLK = 64
NB = 8
LANES = 128
EXT = ROWS + 2 * OHALF
MID = EXT + 2 * HALF
TOP = MID + 2 * HALF
LINES = DEPTHS * EXT
SHARE = LINES // NOFF
F32 = jnp.float32
BF16 = jnp.bfloat16


def lane_ids(shape):
    return lax.broadcasted_iota(jnp.int32, shape, len(shape) - 1)


def block_ids(shape):
    return lax.broadcasted_iota(jnp.int32, shape, len(shape) - 2)


def next_block(x):
    rolled = pltpu.roll(x, NB - 1, x.ndim - 2)
    return jnp.where(block_ids(x.shape) == NB - 1, 0.0, rolled)


def prev_block(x):
    rolled = pltpu.roll(x, 1, x.ndim - 2)
    return jnp.where(block_ids(x.shape) == 0, 0.0, rolled)


def swap_halves(x):
    return pltpu.roll(x, BLK, x.ndim - 1)


def ahead(x, nxt, prv, t):
    if t == 0:
        return x
    j = lane_ids(x.shape) % BLK
    if t > 0:
        return pltpu.roll(jnp.where(j < t, nxt, x), LANES - t, x.ndim - 1)
    return pltpu.roll(jnp.where(j >= BLK + t, prv, x), -t, x.ndim - 1)


def prep_kernel(source, receiver, index, pay, low, high):
    lane = lane_ids((8, LANES))
    planes = (
        (source[0, 0].astype(F32), source[0, 1].astype(F32)),
        (receiver[0, 0].astype(F32), -receiver[0, 1].astype(F32)),
        (index[0].astype(F32), index[1].astype(F32)),
    )
    for p, (one, two) in enumerate(planes):
        for group in range(ROWS // 8):
            rows = slice(8 * group, 8 * group + 8)
            blocks = []
            for g in range(WIDTH // LANES):
                u = one[rows, LANES * g : LANES * g + LANES]
                v = two[rows, LANES * g : LANES * g + LANES]
                blocks.append(jnp.where(lane < BLK, u, swap_halves(v)))
                blocks.append(jnp.where(lane < BLK, swap_halves(u), v))
            turned = jnp.swapaxes(jnp.stack(blocks), 0, 1).astype(BF16)
            pay[rows, 8 * p : 8 * p + 8, :] = turned
            if p < 2:
                subs = slice(8 * p, 8 * p + 8)
                if group == 0:
                    high[0:8, subs, :] = turned
                    low[0:4, subs, :] = turned[4:]
                else:
                    high[8:12, subs, :] = turned[:4]
                    low[4:12, subs, :] = turned


def prep(source, receiver, index):
    return pl.pallas_call(
        prep_kernel,
        out_shape=(
            jax.ShapeDtypeStruct((ROWS, 24, LANES), BF16),
            jax.ShapeDtypeStruct((HALF, 16, LANES), BF16),
            jax.ShapeDtypeStruct((HALF, 16, LANES), BF16),
        ),
        name="prep",
    )(source, receiver, index)


def matrix_kernel(filters, out, base):
    tap = lax.broadcasted_iota(jnp.int32, (FILT, LANES), 0)
    col = lane_ids((FILT, LANES)) % BLK
    perm = ((HALF - tap) % BLK == col).astype(BF16)
    for v in range(NV):
        for part in range(2):
            base[2 * v + part, 0:FILT, :] = jnp.dot(
                filters[0, v, part], perm, preferred_element_type=F32
            )
    lane = lane_ids((BLK, LANES))
    gap = jnp.abs(lax.broadcasted_iota(jnp.int32, (BLK, LANES), 0) - lane % BLK)
    near = gap < BLK // 2

    def one_tap(a, carry):
        for v in range(NV):
            turned = []
            for part in range(2):
                row = base[2 * v + part, pl.ds(a, 1), :]
                full = jnp.broadcast_to(row, (BLK, LANES))
                turned.append(pltpu.roll(full, 0, 1, stride=1, stride_axis=0))
            real, imag = turned
            cols = slice(v * LANES, v * LANES + LANES)
            for c in range(2):
                if c == 0:
                    band = jnp.where(lane < BLK, real, imag)
                else:
                    band = jnp.where(lane < BLK, -imag, real)
                out[a, c * BLK : c * BLK + BLK, cols] = jnp.where(near, band, 0.0).astype(BF16)
                out[a, LANES + c * BLK : LANES + c * BLK + BLK, cols] = jnp.where(
                    near, 0.0, band
                ).astype(BF16)
        return carry

    lax.fori_loop(0, FILT, one_tap, 0)


def filter_matrix(filters):
    return pl.pallas_call(
        matrix_kernel,
        out_shape=jax.ShapeDtypeStruct((FILT, 2 * LANES, 2 * LANES), BF16),
        scratch_shapes=[pltpu.VMEM((2 * NV, 32, LANES), F32)],
        name="matrix",
    )(filters)


CHUNK = 8


def place_rows(buffer, start, rows):
    shape = (rows.shape[0], NB, LANES)
    j = lane_ids(shape) % BLK
    for f in range(2):
        x = rows[:, NB * f : NB * f + NB]
        subs = slice(NB * f, NB * f + NB)
        sides = jnp.where(j < BLK // 2, next_block(x), prev_block(x))
        n = rows.shape[0]
        buffer[start : start + n, subs, 0:LANES] = x.astype(BF16)
        buffer[start : start + n, subs, LANES : 2 * LANES] = sides.astype(BF16)


def filter_rows(buffer, matrix, start):
    acc = None
    for a in range(FILT):
        layer = buffer[start + a : start + a + CHUNK].reshape(CHUNK * 16, 2 * LANES)
        term = jnp.dot(layer, matrix[a], preferred_element_type=F32)
        acc = term if acc is None else acc + term
    return acc.reshape(CHUNK, 16, 2 * LANES)


def pick(acc, mask):
    mask = jnp.concatenate([mask, mask], axis=1)
    return jnp.where(mask == 0.0, acc[:, :, :LANES], acc[:, :, LANES:])


def march_kernel(own, up, down, far_up, far_down, matrix, lines, top, mid):
    here = lax.axis_index("row")
    last = lax.axis_size("row") - 1
    place_rows(top, 0, far_up[...].astype(F32))
    place_rows(top, HALF, up[:, 0:16, :].astype(F32))
    place_rows(top, HALF + ROWS, own[:, 0:16, :].astype(F32))
    place_rows(top, HALF + 2 * ROWS, down[:, 0:16, :].astype(F32))
    place_rows(top, HALF + 3 * ROWS, far_down[...].astype(F32))
    lane = lane_ids((CHUNK, NB, LANES))
    for n in range(MID // CHUNK):
        first = CHUNK * n
        block, inner = divmod(first, ROWS)
        both = (up, own, down)[block][inner : inner + CHUNK, 16:24, :].astype(F32)
        mask = jnp.where(lane < BLK, both, swap_halves(both))
        q = pick(filter_rows(top, matrix, first), mask)
        if block == 0:
            q = jnp.where(here > 0, q, 0.0)
        if block == 2:
            q = jnp.where(here < last, q, 0.0)
        q = q.astype(BF16)
        for i in range(CHUNK):
            line = first + i - HALF
            if 0 <= line < EXT:
                lines[line] = q[i]
        place_rows(mid, first, q.astype(F32))
    for n in range(EXT // CHUNK):
        first = CHUNK * n
        pieces = []
        for i in range(CHUNK):
            block, inner = divmod(first + i + HALF, ROWS)
            pieces.append((up, own, down)[block][inner : inner + 1, 16:24, :].astype(F32))
        both = jnp.concatenate(pieces, axis=0)
        mask = jnp.where(lane < BLK, swap_halves(both), both)
        q = pick(filter_rows(mid, matrix, first), mask)
        for i in range(CHUNK):
            block = (first + i + HALF) // ROWS
            line = q[i]
            if block == 0:
                line = jnp.where(here > 0, line, 0.0)
            if block == 2:
                line = jnp.where(here < last, line, 0.0)
            lines[EXT + first + i] = line.astype(BF16)


def march(own, up, down, far_up, far_down, matrix):
    return pl.pallas_call(
        march_kernel,
        out_shape=jax.ShapeDtypeStruct((LINES, 16, LANES), BF16),
        scratch_shapes=[
            pltpu.VMEM((TOP, 16, 2 * LANES), BF16),
            pltpu.VMEM((MID, 16, 2 * LANES), BF16),
        ],
        name="march",
    )(own, up, down, far_up, far_down, matrix)


def gather_kernel(lags, fields, out, src, rec, rec_next, rec_prev, raw):
    lane = lane_ids((NB, LANES))
    nfreq = fields.shape[0] // SHARE
    for n in range(fields.shape[0]):
        line = fields[n].astype(F32)
        src[n] = line[0:NB]
        r = jnp.where(lane < BLK, line[NB : 2 * NB], -line[NB : 2 * NB])
        rec[n] = r
        flipped = swap_halves(r)
        rec_next[n] = next_block(flipped)
        rec_prev[n] = prev_block(flipped)
    for i in range(NOFF):
        h = i - NOFF // 2
        sums = []
        for m in range(SHARE):
            total = None
            for f in range(nfreq):
                n = f * SHARE + m
                side = rec_next if h > 0 else rec_prev
                term = src[n] * ahead(rec[n], side[n], side[n], 2 * h)
                total = term if total is None else total + term
            total = total + swap_halves(total)
            sums.append(ahead(total, next_block(total), prev_block(total), -h))
        raw[i, 0] = jnp.where(lane < BLK, sums[0], sums[1])
        raw[i, 1] = sums[2]
    for k in range(NOFF):
        out[2 * k : 2 * k + 2] = raw[lags[k]]


def gather_lags(lags, fields):
    n = fields.shape[0]
    return pl.pallas_call(
        gather_kernel,
        out_shape=jax.ShapeDtypeStruct((2 * NOFF, NB, LANES), F32),
        in_specs=[
            pl.BlockSpec(memory_space=pltpu.SMEM),
            pl.BlockSpec(memory_space=pltpu.VMEM),
        ],
        scratch_shapes=[pltpu.VMEM((n, NB, LANES), F32)] * 4
        + [pltpu.VMEM((NOFF, 2, NB, LANES), F32)],
        name="lags",
    )(lags, fields)


def image_kernel(taps, raw, out, rows, nxt, prv):
    lane = lane_ids((NB, LANES))

    def piece(depth, x, high):
        line = depth * EXT + x
        s, m = divmod(line, SHARE)
        got = raw[2 * s + m // 2]
        if m == 2 or (m == 1) == high:
            return got
        return swap_halves(got)

    for x in range(EXT):
        v = jnp.where(lane < BLK, piece(0, x, False), piece(1, x, True))
        rows[x] = v
        flipped = swap_halves(v)
        nxt[x] = next_block(flipped)
        prv[x] = prev_block(flipped)
    for group in range(ROWS // 8):
        accs = [None] * 8
        for b in range(OFILT):
            moved = [
                ahead(rows[8 * group + x], nxt[8 * group + x], prv[8 * group + x], b - OHALF)
                for x in range(8 + 2 * OHALF)
            ]
            for a in range(OFILT):
                w = taps[0, a, b]
                for x in range(8):
                    term = moved[x + a] * w
                    accs[x] = term if accs[x] is None else accs[x] + term
        z = jnp.swapaxes(jnp.stack(accs), 0, 1)
        rows8 = slice(8 * group, 8 * group + 8)
        for g in range(WIDTH // LANES):
            even, odd = z[2 * g], z[2 * g + 1]
            cols = slice(LANES * g, LANES * g + LANES)
            out[0, 0, rows8, cols] = jnp.where(lane < BLK, even, swap_halves(odd))
            out[1, 0, rows8, cols] = jnp.where(lane < BLK, swap_halves(even), odd)


def filter_image(taps, raw):
    return pl.pallas_call(
        image_kernel,
        out_shape=jax.ShapeDtypeStruct((DEPTHS, 1, ROWS, WIDTH), F32),
        in_specs=[
            pl.BlockSpec(memory_space=pltpu.SMEM),
            pl.BlockSpec(memory_space=pltpu.VMEM),
        ],
        scratch_shapes=[pltpu.VMEM((EXT, NB, LANES), F32)] * 3,
        name="image",
    )(taps, raw)


def body(source, receiver, filters, table_index, lags, offset_filters):
    count = lax.axis_size("row")

    def shifted(x, step):
        pairs = [(i, i + step) for i in range(count) if 0 <= i + step < count]
        return lax.ppermute(x, "row", pairs)

    own, low, high = prep(source, receiver, table_index)
    up = shifted(own, 1)
    down = shifted(own, -1)
    far_up = shifted(low, 2)
    far_down = shifted(high, -2)
    matrix = filter_matrix(filters)
    lines = march(own, up, down, far_up, far_down, matrix)
    fields = lax.all_to_all(lines, "freq", 0, 0, tiled=True)
    raw = gather_lags(lags, fields)
    raw = lax.all_to_all(raw, "freq", 0, 0, tiled=True)
    return filter_image(offset_filters, raw)


def solution(mesh):
    in_specs = (
        P("freq", None, "row", None),
        P("freq", None, "row", None),
        P("freq", None, None, None, None),
        P(None, "row", None),
        P(),
        P("freq", None, None),
    )
    out_specs = P(None, "freq", "row", None)
    return jax.shard_map(body, mesh=mesh, in_specs=in_specs, out_specs=out_specs, check_vma=False)
```

time: 433 us -> 70.3 us (0.16)
  the two profiles are of different devices: /device:TPU:224 before, /device:TPU:17 now
where the time goes in v1:
time: 70.3 us; the launch traced here: 69.7 us
  Pallas kernels  23.3 us (33%)
  starting transfers between devices  22.8 us (32%)
  blocking collectives  14.2 us (20%)
  waiting for transfers between devices  5.53 us (8%)
  local copies, waits for them, and re-layouts  3.88 us (6%)
    ppermute x4, starting transfers between devices, shifted(): return lax.ppermute(x, 'row', pairs)  19 us
    all_to_all x1, blocking collectives, body(): fields = lax.all_to_all(lines, 'freq', 0, 0, tiled=True)  14.2 us
    pallas_call x1, Pallas kernels, gather_lags(): pl.pallas_call(gather_kernel, out_shape=jax.ShapeDtypeStruct((2 * NOFF, N...  7.12 us
    pallas_call x1, Pallas kernels, march(): pl.pallas_call(march_kernel, out_shape=jax.ShapeDtypeStruct((LINES, 16, L...  6.83 us
    all_to_all x1, waiting for transfers between devices, body(): raw = lax.all_to_all(raw, 'freq', 0, 0, tiled=True)  5.52 us
    pallas_call x1, Pallas kernels, filter_matrix(): pl.pallas_call(matrix_kernel, out_shape=jax.ShapeDtypeStruct((FILT, 2 * L...  5.46 us
    unnamed x14, local copies, waits for them, and re-layouts  3.88 us
    all_to_all x1, starting transfers between devices, body(): raw = lax.all_to_all(raw, 'freq', 0, 0, tiled=True)  3.83 us
  transfers between devices with their start and end apart: 5, of which 1 were waited for; matrix products, arithmetic and copies ran while one was open for 3% of the time, Pallas kernels for 8%

profile of v1, /device:TPU:17, one launch (start us, length us, event | category | flops | bytes accessed | tf_op | source)
XLA Modules:
  0.0 69.7 jit_solution(5219288079801428582)
XLA Ops:
  0.0 1.7 %prep.1 = (bf16[16,24,128]{2,1,0:T(8,128)(2,1)}, bf16[12,16,128]{2,1,0:T(8,128)(2,1)}, bf16[12,16,128]{2,1,0:T(8,128)(2,1)}) custom-call(bf16[1,2,16,512]{3,2,1,0:T(8,128)(2,1)} %source.1, bf16[1,2,16,512]{3,2,1,0:T(8,128)(2,1)} %receiver.1, s32[2,16,512]{2,1,0:T(8,128)} %index.1), custom_call_target="tpu_custom_call" | custom-call | tf_op jit(solution)/shard_map/prep/pallas_call | solution.py:89
  1.7 3.5 %collective-permute-start = (bf16[16,24,128]{2,1,0:T(8,128)(2,1)}, bf16[16,24,128]{2,1,0:T(8,128)(2,1)S(1)}, u32[]{:S(2)}, u32[]{:S(2)}) collective-permute-start(bf16[16,24,128]{2,1,0:T(8,128)(2,1)} %get-tuple-element.8.own), channel_id=1, source_target_pairs={{0,1},{1,2},{2,3},{3,4},{4,5},{5,6},{6,7},{7,8},{8,9},{9,10},{10,1... | collective-permute-start | bytes 294920 | tf_op jit(solution)/shard_map/ppermute | solution.py:330
  5.2 5.6 %collective-permute-start.1 = (bf16[16,24,128]{2,1,0:T(8,128)(2,1)}, bf16[16,24,128]{2,1,0:T(8,128)(2,1)S(1)}, u32[]{:S(2)}, u32[]{:S(2)}) collective-permute-start(bf16[16,24,128]{2,1,0:T(8,128)(2,1)} %get-tuple-element.8.own), channel_id=1, source_target_pairs={{1,0},{2,1},{3,2},{4,3},{5,4},{6,5},{7,6},{8,7},{9,8},{10,9},{11,1... | collective-permute-start | bytes 294920 | tf_op jit(solution)/shard_map/ppermute | solution.py:330
  10.8 1.9 %collective-permute-start.2 = (bf16[12,16,128]{2,1,0:T(8,128)(2,1)}, bf16[12,16,128]{2,1,0:T(8,128)(2,1)S(1)}, u32[]{:S(2)}, u32[]{:S(2)}) collective-permute-start(bf16[12,16,128]{2,1,0:T(8,128)(2,1)} %get-tuple-element.9), channel_id=1, source_target_pairs={{0,2},{1,3},{2,4},{3,5},{4,6},{5,7},{6,8},{7,9},{8,10},{9,11},{10,... | collective-permute-start | bytes 147464 | tf_op jit(solution)/shard_map/ppermute | solution.py:330
  12.8 7.9 %collective-permute-start.3 = (bf16[12,16,128]{2,1,0:T(8,128)(2,1)}, bf16[12,16,128]{2,1,0:T(8,128)(2,1)S(1)}, u32[]{:S(2)}, u32[]{:S(2)}) collective-permute-start(bf16[12,16,128]{2,1,0:T(8,128)(2,1)} %get-tuple-element.10), channel_id=1, source_target_pairs={{2,0},{3,1},{4,2},{5,3},{6,4},{7,5},{8,6},{9,7},{10,8},{11,9},{12,... | collective-permute-start | bytes 147464 | tf_op jit(solution)/shard_map/ppermute | solution.py:330
  20.6 1.3 %copy.7.filters = bf16[1,2,2,25,25]{4,3,2,1,0:T(8,128)(2,1)} copy(bf16[1,2,2,25,25]{4,2,3,1,0:T(2,128)(2,1)} %param.8) | data formatting | bytes 10000 | tf_op args[2]
  22.0 0.0 copy-start.5
  22.0 5.5 %matrix.1 = bf16[25,256,256]{2,1,0:T(8,128)(2,1)} custom-call(bf16[1,2,2,25,25]{4,3,2,1,0:T(8,128)(2,1)} %copy.7.filters), custom_call_target="tpu_custom_call" | custom-call | tf_op jit(solution)/shard_map/matrix/pallas_call | solution.py:137
  27.5 0.0 collective-permute-done.2.far_up
  27.5 0.0 copy-start.3
  27.5 0.0 collective-permute-done.3.far_down
  27.5 0.0 copy-start.4
  27.5 0.0 collective-permute-done.up
  27.5 0.0 copy-start.1
  27.5 0.0 collective-permute-done.1.down
  27.5 0.6 copy-done.3
  28.1 0.0 copy-done.4
  28.1 0.1 copy-done.1
  28.1 0.0 copy-start.2
  28.1 0.6 copy-done.2
  28.8 6.8 %march.1 = bf16[48,16,128]{2,1,0:T(8,128)(2,1)} custom-call(bf16[16,24,128]{2,1,0:T(8,128)(2,1)} %get-tuple-element.8.own, bf16[16,24,128]{2,1,0:T(8,128)(2,1)} %copy-done.1, bf16[16,24,128]{2,1,0:T(8,128)(2,1)} %copy-done.2, bf16[12,16,128]{2,1,0:T(8,128)(2,1)} %copy-done.3, bf16[12,16,128]{2,1,0:T(8,128)(2,1)} %copy-done.4, bf16[25,256,256]{2,1,0:T(8,128)(2,1)} %matrix.1), custom_call_target="tpu_custom_call" | custom-call | tf_op jit(solution)/shard_map/march/pallas_call | solution.py:219
  35.6 14.2 %all_to_all.10.fields = bf16[48,16,128]{2,1,0:T(8,128)(2,1)} all-to-all(bf16[48,16,128]{2,1,0:T(8,128)(2,1)} %march.1), channel_id=1, replica_groups=mesh['freq'=16,'row'=16] {'freq'}, dimensions={0} | all-to-all | bytes 393216 | tf_op jit(solution)/shard_map/all_to_all | solution.py:339
  49.8 7.1 %lags.2 = f32[32,8,128]{2,1,0:T(8,128)} custom-call(s32[16]{0:T(128)} %lags.3, bf16[48,16,128]{2,1,0:T(8,128)(2,1)} %all_to_all.10.fields), custom_call_target="tpu_custom_call" | custom-call | tf_op jit(solution)/shard_map/lags/pallas_call | solution.py:261
  56.9 3.8 %all-to-all-start.1 = ((f32[32,8,128]{2,1,0:T(8,128)}), f32[32,8,128]{2,1,0:T(8,128)S(1)}, u32[]{:S(2)}, u32[]{:S(2)}) async-start(f32[32,8,128]{2,1,0:T(8,128)} %lags.2), calls=%async_computation.1 | async-start | bytes 262144 | tf_op jit(solution)/shard_map/all_to_all | solution.py:341
  60.7 0.0 copy-done.5
  60.7 0.6 copy.8.taps
  61.3 5.5 %all-to-all-done.1.raw = f32[32,8,128]{2,1,0:T(8,128)S(1)} async-done(((f32[32,8,128]{2,1,0:T(8,128)}), f32[32,8,128]{2,1,0:T(8,128)S(1)}, u32[]{:S(2)}, u32[]{:S(2)}) %all-to-all-start.1) | async-done | bytes 131104 | tf_op jit(solution)/shard_map/all_to_all | solution.py:341
  66.9 0.0 copy-start
  66.9 0.6 copy-done
  67.5 2.2 %image.1 = f32[2,1,16,512]{3,2,1,0:T(8,128)} custom-call(f32[1,9,9]{2,1,0:T(8,128)} %copy.8.taps, f32[32,8,128]{2,1,0:T(8,128)} %copy-done), custom_call_target="tpu_custom_call" | custom-call | tf_op jit(solution)/shard_map/image/pallas_call | solution.py:313
Async XLA Ops:
  1.7 25.8 %collective-permute-start = (bf16[16,24,128]{2,1,0:T(8,128)(2,1)}, bf16[16,24,128]{2,1,0:T(8,128)(2,1)S(1)}, u32[]{:S(2)}, u32[]{:S(2)}) collective-permute-start(bf16[16,24,128]{2,1,0:T(8,128)(2,1)} %get-tuple-element.8.own), channel_id=1, source_target_pairs={{0,1},{1,2},{2,3},{3,4},{4,5},{5,6},{6,7},{7,8},{8,9},{9,10},{10,1... | collective-permute-start | bytes 294920 | tf_op jit(solution)/shard_map/ppermute | solution.py:330
  5.2 22.3 %collective-permute-start.1 = (bf16[16,24,128]{2,1,0:T(8,128)(2,1)}, bf16[16,24,128]{2,1,0:T(8,128)(2,1)S(1)}, u32[]{:S(2)}, u32[]{:S(2)}) collective-permute-start(bf16[16,24,128]{2,1,0:T(8,128)(2,1)} %get-tuple-element.8.own), channel_id=1, source_target_pairs={{1,0},{2,1},{3,2},{4,3},{5,4},{6,5},{7,6},{8,7},{9,8},{10,9},{11,1... | collective-permute-start | bytes 294920 | tf_op jit(solution)/shard_map/ppermute | solution.py:330
  10.8 16.6 %collective-permute-start.2 = (bf16[12,16,128]{2,1,0:T(8,128)(2,1)}, bf16[12,16,128]{2,1,0:T(8,128)(2,1)S(1)}, u32[]{:S(2)}, u32[]{:S(2)}) collective-permute-start(bf16[12,16,128]{2,1,0:T(8,128)(2,1)} %get-tuple-element.9), channel_id=1, source_target_pairs={{0,2},{1,3},{2,4},{3,5},{4,6},{5,7},{6,8},{7,9},{8,10},{9,11},{10,... | collective-permute-start | bytes 147464 | tf_op jit(solution)/shard_map/ppermute | solution.py:330
  12.8 14.7 %collective-permute-start.3 = (bf16[12,16,128]{2,1,0:T(8,128)(2,1)}, bf16[12,16,128]{2,1,0:T(8,128)(2,1)S(1)}, u32[]{:S(2)}, u32[]{:S(2)}) collective-permute-start(bf16[12,16,128]{2,1,0:T(8,128)(2,1)} %get-tuple-element.10), channel_id=1, source_target_pairs={{2,0},{3,1},{4,2},{5,3},{6,4},{7,5},{8,6},{9,7},{10,8},{11,9},{12,... | collective-permute-start | bytes 147464 | tf_op jit(solution)/shard_map/ppermute | solution.py:330
  22.0 38.7 %copy-start.5 = (f32[1,9,9]{2,0,1:T(1,128)S(1)}, f32[1,9,9]{2,0,1:T(1,128)}, u32[]{:S(2)}) copy-start(f32[1,9,9]{2,0,1:T(1,128)} %param.11) | copy-start | bytes 976
  27.5 0.6 copy-start.3
  27.5 0.6 copy-start.4
  27.5 0.7 copy-start.1
  28.1 0.6 copy-start.2
  56.9 10.0 %all-to-all-start.1 = ((f32[32,8,128]{2,1,0:T(8,128)}), f32[32,8,128]{2,1,0:T(8,128)S(1)}, u32[]{:S(2)}, u32[]{:S(2)}) async-start(f32[32,8,128]{2,1,0:T(8,128)} %lags.2), calls=%async_computation.1 | async-start | bytes 262144 | tf_op jit(solution)/shard_map/all_to_all | solution.py:341
  66.9 0.7 copy-start

commit v2 on v1

v2 whole, which is shorter than its diff:
```python
import jax
import jax.numpy as jnp
import numpy as np
from jax import lax
from jax.experimental import pallas as pl
from jax.experimental.pallas import tpu as pltpu
from jax.sharding import PartitionSpec as P

NV = 2
FILT = 25
HALF = 12
NOFF = 16
OFILT = 9
OHALF = 4
DEPTHS = 2
ROWS = 16
WIDTH = 512
BLK = 64
NB = 8
LANES = 128
EXT = ROWS + 2 * OHALF
MID = EXT + 2 * HALF
LINES = DEPTHS * EXT
SHARE = LINES // NOFF
F32 = jnp.float32
BF16 = jnp.bfloat16


def lane_ids(shape):
    return lax.broadcasted_iota(jnp.int32, shape, len(shape) - 1)


def block_ids(shape):
    return lax.broadcasted_iota(jnp.int32, shape, len(shape) - 2)


def next_block(x):
    rolled = pltpu.roll(x, NB - 1, x.ndim - 2)
    return jnp.where(block_ids(x.shape) == NB - 1, 0.0, rolled)


def prev_block(x):
    rolled = pltpu.roll(x, 1, x.ndim - 2)
    return jnp.where(block_ids(x.shape) == 0, 0.0, rolled)


def swap_halves(x):
    return pltpu.roll(x, BLK, x.ndim - 1)


def ahead(x, nxt, prv, t):
    if t == 0:
        return x
    j = lane_ids(x.shape) % BLK
    if t > 0:
        return pltpu.roll(jnp.where(j < t, nxt, x), LANES - t, x.ndim - 1)
    return pltpu.roll(jnp.where(j >= BLK + t, prv, x), -t, x.ndim - 1)


def prep_kernel(source, receiver, index, own, south, north):
    lane = lane_ids((8, LANES))
    planes = (
        (source[0, 0].astype(F32), source[0, 1].astype(F32)),
        (receiver[0, 0].astype(F32), -receiver[0, 1].astype(F32)),
        (index[0].astype(F32), index[1].astype(F32)),
    )
    for p, (one, two) in enumerate(planes):
        for group in range(ROWS // 8):
            rows = slice(8 * group, 8 * group + 8)
            blocks = []
            for g in range(WIDTH // LANES):
                u = one[rows, LANES * g : LANES * g + LANES]
                v = two[rows, LANES * g : LANES * g + LANES]
                blocks.append(jnp.where(lane < BLK, u, swap_halves(v)))
                blocks.append(jnp.where(lane < BLK, swap_halves(u), v))
            turned = jnp.swapaxes(jnp.stack(blocks), 0, 1).astype(BF16)
            subs = slice(8 * p, 8 * p + 8)
            own[rows, subs, :] = turned
            if p < 2:
                south[rows, subs, :] = turned
                north[rows, subs, :] = turned
            else:
                dest, base = (north, 0) if group == 0 else (south, 4)
                for i in range(OHALF):
                    dest[ROWS + i // 2, 8 * (i % 2) : 8 * (i % 2) + 8, :] = turned[base + i]


def in_vmem(*arrays):
    return [pltpu.with_memory_space_constraint(x, pltpu.VMEM) for x in arrays]


PARAMS = pltpu.CompilerParams(vmem_limit_bytes=12 << 20)
VSPEC = pl.BlockSpec(memory_space=pltpu.VMEM)
SSPEC = pl.BlockSpec(memory_space=pltpu.SMEM)


def prep(source, receiver, index):
    send = pltpu.VMEM((ROWS + 2, 16, LANES), BF16)
    return pl.pallas_call(
        prep_kernel,
        out_shape=(pltpu.VMEM((ROWS, 24, LANES), BF16), send, send),
        out_specs=(VSPEC, VSPEC, VSPEC),
        compiler_params=PARAMS,
        name="prep",
    )(source, receiver, index)


def matrix_kernel(filters, out, base):
    tap = lax.broadcasted_iota(jnp.int32, (FILT, LANES), 0)
    col = lane_ids((FILT, LANES)) % BLK
    perm = ((HALF - tap) % BLK == col).astype(BF16)
    for v in range(NV):
        for part in range(2):
            base[2 * v + part, 0:FILT, :] = jnp.dot(
                filters[0, v, part], perm, preferred_element_type=F32
            )
    lane = lane_ids((16, LANES))
    row = lax.broadcasted_iota(jnp.int32, (16, LANES), 0)
    zero = jnp.zeros((16, LANES), BF16)

    def one_tap(a):
        for v in range(NV):
            turned = []
            for part in range(2):
                taps = jnp.broadcast_to(base[2 * v + part, pl.ds(a, 1), :], (BLK, LANES))
                turned.append(pltpu.roll(taps, 0, 1, stride=1, stride_axis=0))
            cols = slice(v * LANES, v * LANES + LANES)
            for top in range(0, BLK, 16):
                real, imag = (x[top : top + 16] for x in turned)
                near = jnp.abs(row + top - lane % BLK) < BLK // 2
                for c in range(2):
                    if c == 0:
                        band = jnp.where(lane < BLK, real, imag)
                    else:
                        band = jnp.where(lane < BLK, -imag, real)
                    at = c * BLK + top
                    if top in (0, BLK - 16):
                        out[a, at : at + 16, cols] = jnp.where(near, band, 0.0).astype(BF16)
                        at += LANES
                        out[a, at : at + 16, cols] = jnp.where(near, 0.0, band).astype(BF16)
                    else:
                        out[a, at : at + 16, cols] = band.astype(BF16)
                        at += LANES
                        out[a, at : at + 16, cols] = zero

    for a in range(FILT):
        one_tap(a)


def filter_matrix(filters):
    return pl.pallas_call(
        matrix_kernel,
        out_shape=pltpu.VMEM((FILT, 2 * LANES, 2 * LANES), BF16),
        out_specs=VSPEC,
        scratch_shapes=[pltpu.VMEM((2 * NV, 32, LANES), F32)],
        compiler_params=PARAMS,
        name="matrix",
    )(filters)


def place_rows(buffer, start, rows):
    n = rows.shape[0]
    j = lane_ids((n, NB, LANES)) % BLK
    for f in range(2):
        subs = slice(NB * f, NB * f + NB)
        x = rows[:, subs]
        sides = jnp.where(j < BLK // 2, next_block(x), prev_block(x))
        buffer[start : start + n, subs, 0:LANES] = x.astype(BF16)
        buffer[start : start + n, subs, LANES : 2 * LANES] = sides.astype(BF16)


def filter_rows(buffer, matrix):
    acc = None
    for a in range(FILT):
        layer = buffer[a : a + EXT].reshape(EXT * 16, 2 * LANES)
        term = jnp.dot(layer, matrix[a], preferred_element_type=F32)
        acc = term if acc is None else acc + term
    return acc.reshape(EXT, 16, 2 * LANES)


def pick(acc, own, up, down, depth):
    here = lax.axis_index("row")
    last = lax.axis_size("row") - 1
    lane = lane_ids((NB, LANES))
    rows = []
    for x in range(EXT):
        i = x - OHALF
        if 0 <= i < ROWS:
            both = own[i, 16:24, :].astype(F32)
        else:
            i = x % ROWS
            pack = up if x < OHALF else down
            i = i % OHALF
            both = pack[ROWS + i // 2, 8 * (i % 2) : 8 * (i % 2) + 8, :].astype(F32)
        swapped = swap_halves(both)
        mask = jnp.where(lane < BLK, both, swapped) if depth == 0 else jnp.where(lane < BLK, swapped, both)
        mask = jnp.concatenate([mask, mask], axis=0)
        q = jnp.where(mask == 0.0, acc[x, :, :LANES], acc[x, :, LANES:])
        if x < OHALF:
            q = jnp.where(here > 0, q, 0.0)
        if x >= OHALF + ROWS:
            q = jnp.where(here < last, q, 0.0)
        rows.append(q.astype(BF16))
    return rows


def first_kernel(own, up, down, matrix, lines, south, north, top):
    here = lax.axis_index("row")
    last = lax.axis_size("row") - 1
    place_rows(top, 0, jnp.where(here > 0, up[0:ROWS].astype(F32), 0.0))
    place_rows(top, ROWS, own[:, 0:16, :].astype(F32))
    place_rows(top, 2 * ROWS, jnp.where(here < last, down[0:ROWS].astype(F32), 0.0))
    rows = pick(filter_rows(top, matrix), own, up, down, 0)
    for x, q in enumerate(rows):
        lines[x] = q
        i = x - OHALF
        if 0 <= i < HALF:
            north[i] = q
        if ROWS - HALF <= i < ROWS:
            south[i - OHALF] = q


def first_step(own, up, down, matrix):
    send = pltpu.VMEM((HALF, 16, LANES), BF16)
    return pl.pallas_call(
        first_kernel,
        out_shape=(pltpu.VMEM((EXT, 16, LANES), BF16), send, send),
        in_specs=[VSPEC] * 4,
        out_specs=(VSPEC,) * 3,
        scratch_shapes=[pltpu.VMEM((MID, 16, 2 * LANES), BF16)],
        compiler_params=PARAMS,
        name="first",
    )(*in_vmem(own, up, down, matrix))


def second_kernel(own, up, down, matrix, done, above, below, lines, mid):
    here = lax.axis_index("row")
    last = lax.axis_size("row") - 1
    place_rows(mid, 0, jnp.where(here > 0, above[...].astype(F32), 0.0))
    place_rows(mid, HALF, done[...].astype(F32))
    place_rows(mid, HALF + EXT, jnp.where(here < last, below[...].astype(F32), 0.0))
    lines[0:EXT] = done[...]
    rows = pick(filter_rows(mid, matrix), own, up, down, 1)
    for x, q in enumerate(rows):
        lines[EXT + x] = q


def second_step(own, up, down, matrix, done, above, below):
    return pl.pallas_call(
        second_kernel,
        out_shape=pltpu.VMEM((LINES, 16, LANES), BF16),
        in_specs=[VSPEC] * 7,
        out_specs=VSPEC,
        scratch_shapes=[pltpu.VMEM((MID, 16, 2 * LANES), BF16)],
        compiler_params=PARAMS,
        name="second",
    )(*in_vmem(own, up, down, matrix, done, above, below))


def shift_table():
    k = np.arange(2 * LANES)[:, None]
    n = np.arange(NOFF * LANES)[None, :]
    group, c, j = k // LANES, k % LANES // BLK, k % BLK
    want = n % BLK + 2 * (n // LANES - NOFF // 2)
    same = (n % LANES // BLK == c) & (want % BLK == j)
    inside = (want >= 0) & (want < BLK)
    sign = np.where(c == 0, 1.0, -1.0)
    return (same & (inside == (group == 0))) * sign


def gather_kernel(lags, fields, table, out, src, rec, raw):
    lane = lane_ids((NB, LANES))
    j = lane % BLK
    nfreq = fields.shape[0] // SHARE
    for n in range(fields.shape[0]):
        f, m = divmod(n, SHARE)
        line = fields[n].astype(F32)
        src[m, NB * f : NB * f + NB, :] = line[0:NB]
        r = line[NB : 2 * NB]
        sides = jnp.where(j < BLK // 2, next_block(r), prev_block(r))
        rec[m, NB * f : NB * f + NB, 0:LANES] = r.astype(BF16)
        rec[m, NB * f : NB * f + NB, LANES : 2 * LANES] = sides.astype(BF16)
    for i in range(0, NOFF, 2):
        sums = [[], []]
        for m in range(SHARE):
            moved = jnp.dot(
                rec[m], table[:, LANES * i : LANES * i + 2 * LANES], preferred_element_type=F32
            )
            for e in range(2):
                h = i + e - NOFF // 2
                term = (moved[:, LANES * e : LANES * e + LANES] * src[m]).reshape(nfreq, NB, LANES)
                total = jnp.sum(term, axis=0)
                total = total + swap_halves(total)
                sums[e].append(ahead(total, next_block(total), prev_block(total), -h))
        for e in range(2):
            raw[i + e, 0] = jnp.where(lane < BLK, sums[e][0], sums[e][1])
            raw[i + e, 1] = sums[e][2]
    for k in range(NOFF):
        out[2 * k : 2 * k + 2] = raw[lags[k]]


def gather_lags(lags, fields):
    nfreq = fields.shape[0] // SHARE
    table = jnp.asarray(shift_table(), BF16)
    return pl.pallas_call(
        gather_kernel,
        out_shape=pltpu.VMEM((2 * NOFF, NB, LANES), F32),
        in_specs=[SSPEC, VSPEC, VSPEC],
        out_specs=VSPEC,
        scratch_shapes=[
            pltpu.VMEM((SHARE, NB * nfreq, LANES), F32),
            pltpu.VMEM((SHARE, NB * nfreq, 2 * LANES), BF16),
            pltpu.VMEM((NOFF, 2, NB, LANES), F32),
        ],
        compiler_params=PARAMS,
        name="lags",
    )(lags, *in_vmem(fields, table))


def image_kernel(taps, raw, out, rows, nxt, prv):
    lane = lane_ids((NB, LANES))

    def piece(depth, x, high):
        line = depth * EXT + x
        s, m = divmod(line, SHARE)
        got = raw[2 * s + m // 2]
        if m == 2 or (m == 1) == high:
            return got
        return swap_halves(got)

    for x in range(EXT):
        v = jnp.where(lane < BLK, piece(0, x, False), piece(1, x, True))
        rows[x] = v
        flipped = swap_halves(v)
        nxt[x] = next_block(flipped)
        prv[x] = prev_block(flipped)
    for group in range(ROWS // 8):
        accs = [None] * 8
        for b in range(OFILT):
            moved = [
                ahead(rows[8 * group + x], nxt[8 * group + x], prv[8 * group + x], b - OHALF)
                for x in range(8 + 2 * OHALF)
            ]
            for a in range(OFILT):
                w = taps[0, a, b]
                for x in range(8):
                    term = moved[x + a] * w
                    accs[x] = term if accs[x] is None else accs[x] + term
        z = jnp.swapaxes(jnp.stack(accs), 0, 1)
        rows8 = slice(8 * group, 8 * group + 8)
        for g in range(WIDTH // LANES):
            even, odd = z[2 * g], z[2 * g + 1]
            cols = slice(LANES * g, LANES * g + LANES)
            out[0, 0, rows8, cols] = jnp.where(lane < BLK, even, swap_halves(odd))
            out[1, 0, rows8, cols] = jnp.where(lane < BLK, swap_halves(even), odd)


def filter_image(taps, raw):
    return pl.pallas_call(
        image_kernel,
        out_shape=jax.ShapeDtypeStruct((DEPTHS, 1, ROWS, WIDTH), F32),
        in_specs=[SSPEC, VSPEC],
        scratch_shapes=[pltpu.VMEM((EXT, NB, LANES), F32)] * 3,
        compiler_params=PARAMS,
        name="image",
    )(taps, *in_vmem(raw))


def body(source, receiver, filters, table_index, lags, offset_filters):
    count = lax.axis_size("row")

    def shifted(x, step):
        return lax.ppermute(x, "row", [(i, (i + step) % count) for i in range(count)])

    own, south, north = prep(source, receiver, table_index)
    up = shifted(south, 1)
    down = shifted(north, -1)
    matrix = filter_matrix(filters)
    done, south, north = first_step(own, up, down, matrix)
    above = shifted(north, 1)
    below = shifted(south, -1)
    lines = second_step(own, up, down, matrix, done, above, below)
    fields = lax.all_to_all(lines, "freq", 0, 0, tiled=True)
    raw = gather_lags(lags, fields)
    raw = lax.all_to_all(raw, "freq", 0, 0, tiled=True)
    return filter_image(offset_filters, raw)


def solution(mesh):
    in_specs = (
        P("freq", None, "row", None),
        P("freq", None, "row", None),
        P("freq", None, None, None, None),
        P(None, "row", None),
        P(),
        P("freq", None, None),
    )
    out_specs = P(None, "freq", "row", None)
    return jax.shard_map(body, mesh=mesh, in_specs=in_specs, out_specs=out_specs, check_vma=False)
```

time: 70.3 us -> 50.8 us (0.72)
  the two profiles are of different devices: /device:TPU:17 before, /device:TPU:1 now
where the time goes in v2:
time: 50.8 us; the launch traced here: 50.4 us
  starting transfers between devices  18.3 us (36%)
  blocking collectives  13.5 us (27%)
  Pallas kernels  7.88 us (16%)
  waiting for transfers between devices  7.51 us (15%)
  local copies, waits for them, and re-layouts  3.12 us (6%)
    ppermute x4, starting transfers between devices, shifted(): lax.ppermute(x, 'row', [(i, (i + step) % count) for i in range(count)])  14.4 us
    all_to_all x1, blocking collectives, body(): fields = lax.all_to_all(lines, 'freq', 0, 0, tiled=True)  13.5 us
    all_to_all x1, waiting for transfers between devices, body(): raw = lax.all_to_all(raw, 'freq', 0, 0, tiled=True)  6.11 us
    all_to_all x1, starting transfers between devices, body(): raw = lax.all_to_all(raw, 'freq', 0, 0, tiled=True)  3.84 us
    unnamed x14, local copies, waits for them, and re-layouts  3.12 us
    pallas_call x1, Pallas kernels, filter_image(): pl.pallas_call(image_kernel, out_shape=jax.ShapeDtypeStruct((DEPTHS, 1, R...  1.96 us
    pallas_call x1, Pallas kernels, gather_lags(): pl.pallas_call(gather_kernel, out_shape=pltpu.VMEM((2 * NOFF, NB, LANES),...  1.95 us
    pallas_call x1, Pallas kernels, second_step(): pl.pallas_call(second_kernel, out_shape=pltpu.VMEM((LINES, 16, LANES), BF...  1.45 us
  transfers between devices with their start and end apart: 5, of which 2 were waited for; matrix products, arithmetic and copies ran while one was open for 1% of the time, Pallas kernels for 2%

profile of v2, /device:TPU:1, one launch (start us, length us, event | category | flops | bytes accessed | tf_op | source)
XLA Modules:
  0.0 50.4 jit_solution(9164947855019081455)
XLA Ops:
  0.0 0.0 copy-start.1
  0.0 0.8 %copy-done.1 = s32[2,16,512]{2,1,0:T(8,128)S(1)} copy-done((s32[2,16,512]{2,1,0:T(8,128)S(1)}, s32[2,16,512]{2,1,0:T(8,128)}, u32[]{:S(2)}) %copy-start.1) | copy-done | bytes 65560
  0.8 0.0 copy-start.2
  0.8 0.8 %copy-done.2 = bf16[1,2,16,512]{3,2,1,0:T(8,128)(2,1)S(1)} copy-done((bf16[1,2,16,512]{3,2,1,0:T(8,128)(2,1)S(1)}, bf16[1,2,16,512]{3,2,1,0:T(8,128)(2,1)}, u32[]{:S(2)}) %copy-start.2) | copy-done | bytes 32792
  1.6 0.0 copy-start.3
  1.6 0.8 %copy-done.3 = bf16[1,2,16,512]{3,2,1,0:T(8,128)(2,1)S(1)} copy-done((bf16[1,2,16,512]{3,2,1,0:T(8,128)(2,1)S(1)}, bf16[1,2,16,512]{3,2,1,0:T(8,128)(2,1)}, u32[]{:S(2)}) %copy-start.3) | copy-done | bytes 32792
  2.4 0.1 prep.1
  2.5 2.5 %collective-permute-start = (bf16[18,16,128]{2,1,0:T(8,128)(2,1)S(1)}, bf16[18,16,128]{2,1,0:T(8,128)(2,1)S(1)}, u32[]{:S(2)}, u32[]{:S(2)}) collective-permute-start(bf16[18,16,128]{2,1,0:T(8,128)(2,1)S(1)} %get-tuple-element.12), channel_id=1, source_target_pairs={{0,1},{1,2},{2,3},{3,4},{4,5},{5,6},{6,7},{7,8},{8,9},{9,10},{10,1... | collective-permute-start | bytes 221192 | tf_op jit(solution)/shard_map/ppermute | solution.py:373
  5.0 6.7 %collective-permute-start.1 = (bf16[18,16,128]{2,1,0:T(8,128)(2,1)S(1)}, bf16[18,16,128]{2,1,0:T(8,128)(2,1)S(1)}, u32[]{:S(2)}, u32[]{:S(2)}) collective-permute-start(bf16[18,16,128]{2,1,0:T(8,128)(2,1)S(1)} %get-tuple-element.13), channel_id=1, source_target_pairs={{0,15},{1,0},{2,1},{3,2},{4,3},{5,4},{6,5},{7,6},{8,7},{9,8},{10,9... | collective-permute-start | bytes 221192 | tf_op jit(solution)/shard_map/ppermute | solution.py:373
  11.7 0.7 %copy.8.filters = bf16[1,2,2,25,25]{4,3,2,1,0:T(8,128)(2,1)S(1)} copy(bf16[1,2,2,25,25]{4,2,3,1,0:T(2,128)(2,1)} %param.9) | data formatting | bytes 10000 | tf_op args[2]
  12.4 0.9 %matrix.1 = bf16[25,256,256]{2,1,0:T(8,128)(2,1)S(1)} custom-call(bf16[1,2,2,25,25]{4,3,2,1,0:T(8,128)(2,1)S(1)} %copy.8.filters), custom_call_target="tpu_custom_call" | custom-call | tf_op jit(solution)/shard_map/matrix/pallas_call | solution.py:151
  13.4 0.0 collective-permute-done.up
  13.4 0.0 collective-permute-done.1.down
  13.4 0.0 copy-start
  13.4 0.0 copy-start.4
  13.4 1.4 %first.1 = (bf16[24,16,128]{2,1,0:T(8,128)(2,1)S(1)}, bf16[12,16,128]{2,1,0:T(8,128)(2,1)S(1)}, bf16[12,16,128]{2,1,0:T(8,128)(2,1)S(1)}) custom-call(bf16[16,24,128]{2,1,0:T(8,128)(2,1)S(1)} %get-tuple-element.11.own, bf16[18,16,128]{2,1,0:T(8,128)(2,1)S(1)} %collective-permute-done.up, bf16[18,16,128]{2,1,0:T(8,128)(2,1)S(1)} %collective-permute-done.1.down, ...), custom_call_target="tpu_custom_call" | custom-call | tf_op jit(solution)/shard_map/first/pallas_call | solution.py:225
  14.9 0.0 copy-start.5
  14.9 0.1 collective-permute-start.2
  15.0 5.1 %collective-permute-start.3 = (bf16[12,16,128]{2,1,0:T(8,128)(2,1)S(1)}, bf16[12,16,128]{2,1,0:T(8,128)(2,1)S(1)}, u32[]{:S(2)}, u32[]{:S(2)}) collective-permute-start(bf16[12,16,128]{2,1,0:T(8,128)(2,1)S(1)} %get-tuple-element.16), channel_id=1, source_target_pairs={{0,15},{1,0},{2,1},{3,2},{4,3},{5,4},{6,5},{7,6},{8,7},{9,8},{10,9... | collective-permute-start | bytes 147464 | tf_op jit(solution)/shard_map/ppermute | solution.py:373
  20.1 1.4 %collective-permute-done.2.above = bf16[12,16,128]{2,1,0:T(8,128)(2,1)S(1)} collective-permute-done((bf16[12,16,128]{2,1,0:T(8,128)(2,1)S(1)}, bf16[12,16,128]{2,1,0:T(8,128)(2,1)S(1)}, u32[]{:S(2)}, u32[]{:S(2)}) %collective-permute-start.2) | collective-permute-done | bytes 49184 | tf_op jit(solution)/shard_map/ppermute | solution.py:373
  21.5 0.0 collective-permute-done.3.below
  21.5 1.4 %second.1 = bf16[48,16,128]{2,1,0:T(8,128)(2,1)S(1)} custom-call(bf16[16,24,128]{2,1,0:T(8,128)(2,1)S(1)} %get-tuple-element.11.own, bf16[18,16,128]{2,1,0:T(8,128)(2,1)S(1)} %collective-permute-done.up, bf16[18,16,128]{2,1,0:T(8,128)(2,1)S(1)} %collective-permute-done.1.down, bf16[25,256,256]{2,1,0:T(8,128)(2,1)S(1)} %matrix.1, ...), custom_call_target="tpu_custom_call" | custom-call | tf_op jit(solution)/shard_map/second/pallas_call | solution.py:249
  23.0 13.5 %all_to_all.10.fields = bf16[48,16,128]{2,1,0:T(8,128)(2,1)S(1)} all-to-all(bf16[48,16,128]{2,1,0:T(8,128)(2,1)S(1)} %second.1), channel_id=1, replica_groups=mesh['freq'=16,'row'=16] {'freq'}, dimensions={0} | all-to-all | bytes 393216 | tf_op jit(solution)/shard_map/all_to_all | solution.py:383
  36.5 0.0 copy-done
  36.5 0.0 copy-done.4
  36.5 1.9 %lags.2 = f32[32,8,128]{2,1,0:T(8,128)} custom-call(s32[16]{0:T(128)S(1)} %copy-done.4, bf16[48,16,128]{2,1,0:T(8,128)(2,1)S(1)} %all_to_all.10.fields, bf16[256,2048]{1,0:T(8,128)(2,1)S(1)} %copy-done), custom_call_target="tpu_custom_call" | custom-call | tf_op jit(solution)/shard_map/lags/pallas_call | solution.py:305
  38.5 3.8 %all-to-all-start.1 = ((f32[32,8,128]{2,1,0:T(8,128)}), f32[32,8,128]{2,1,0:T(8,128)S(1)}, u32[]{:S(2)}, u32[]{:S(2)}) async-start(f32[32,8,128]{2,1,0:T(8,128)} %lags.2), calls=%async_computation.1 | async-start | bytes 262144 | tf_op jit(solution)/shard_map/all_to_all | solution.py:385
  42.3 0.0 copy-done.5
  42.3 6.1 %all-to-all-done.1.raw = f32[32,8,128]{2,1,0:T(8,128)S(1)} async-done(((f32[32,8,128]{2,1,0:T(8,128)}), f32[32,8,128]{2,1,0:T(8,128)S(1)}, u32[]{:S(2)}, u32[]{:S(2)}) %all-to-all-start.1) | async-done | bytes 131104 | tf_op jit(solution)/shard_map/all_to_all | solution.py:385
  48.4 2.0 %image.1 = f32[2,1,16,512]{3,2,1,0:T(8,128)} custom-call(f32[1,9,9]{2,1,0:T(8,128)S(1)} %copy.9.taps, f32[32,8,128]{2,1,0:T(8,128)S(1)} %all-to-all-done.1.raw), custom_call_target="tpu_custom_call" | custom-call | tf_op jit(solution)/shard_map/image/pallas_call | solution.py:359
  (1 shorter events, 0.0 us)
Async XLA Ops:
  0.0 0.8 %copy-start.1 = (s32[2,16,512]{2,1,0:T(8,128)S(1)}, s32[2,16,512]{2,1,0:T(8,128)}, u32[]{:S(2)}) copy-start(s32[2,16,512]{2,1,0:T(8,128)} %index.1) | copy-start | bytes 196612
  0.8 0.8 %copy-start.2 = (bf16[1,2,16,512]{3,2,1,0:T(8,128)(2,1)S(1)}, bf16[1,2,16,512]{3,2,1,0:T(8,128)(2,1)}, u32[]{:S(2)}) copy-start(bf16[1,2,16,512]{3,2,1,0:T(8,128)(2,1)} %source.1) | copy-start | bytes 98308
  1.6 0.8 %copy-start.3 = (bf16[1,2,16,512]{3,2,1,0:T(8,128)(2,1)S(1)}, bf16[1,2,16,512]{3,2,1,0:T(8,128)(2,1)}, u32[]{:S(2)}) copy-start(bf16[1,2,16,512]{3,2,1,0:T(8,128)(2,1)} %receiver.1) | copy-start | bytes 98308
  2.5 10.9 %collective-permute-start = (bf16[18,16,128]{2,1,0:T(8,128)(2,1)S(1)}, bf16[18,16,128]{2,1,0:T(8,128)(2,1)S(1)}, u32[]{:S(2)}, u32[]{:S(2)}) collective-permute-start(bf16[18,16,128]{2,1,0:T(8,128)(2,1)S(1)} %get-tuple-element.12), channel_id=1, source_target_pairs={{0,1},{1,2},{2,3},{3,4},{4,5},{5,6},{6,7},{7,8},{8,9},{9,10},{10,1... | collective-permute-start | bytes 221192 | tf_op jit(solution)/shard_map/ppermute | solution.py:373
  5.0 8.4 %collective-permute-start.1 = (bf16[18,16,128]{2,1,0:T(8,128)(2,1)S(1)}, bf16[18,16,128]{2,1,0:T(8,128)(2,1)S(1)}, u32[]{:S(2)}, u32[]{:S(2)}) collective-permute-start(bf16[18,16,128]{2,1,0:T(8,128)(2,1)S(1)} %get-tuple-element.13), channel_id=1, source_target_pairs={{0,15},{1,0},{2,1},{3,2},{4,3},{5,4},{6,5},{7,6},{8,7},{9,8},{10,9... | collective-permute-start | bytes 221192 | tf_op jit(solution)/shard_map/ppermute | solution.py:373
  13.4 23.1 %copy-start = (bf16[256,2048]{1,0:T(8,128)(2,1)S(1)}, bf16[256,2048]{1,0:T(8,128)(2,1)}, u32[]{:S(2)}) copy-start(bf16[256,2048]{1,0:T(8,128)(2,1)} %constant.2.clone.table) | copy-start | bytes 3145732
  13.4 23.1 %copy-start.4 = (s32[16]{0:T(128)S(1)}, s32[16]{0:T(128)}, u32[]{:S(2)}) copy-start(s32[16]{0:T(128)} %lags.3) | copy-start | bytes 196
  14.9 27.4 %copy-start.5 = (f32[1,9,9]{2,0,1:T(1,128)S(1)}, f32[1,9,9]{2,0,1:T(1,128)}, u32[]{:S(2)}) copy-start(f32[1,9,9]{2,0,1:T(1,128)} %param.12) | copy-start | bytes 976
  14.9 6.6 %collective-permute-start.2 = (bf16[12,16,128]{2,1,0:T(8,128)(2,1)S(1)}, bf16[12,16,128]{2,1,0:T(8,128)(2,1)S(1)}, u32[]{:S(2)}, u32[]{:S(2)}) collective-permute-start(bf16[12,16,128]{2,1,0:T(8,128)(2,1)S(1)} %get-tuple-element.15), channel_id=1, source_target_pairs={{0,1},{1,2},{2,3},{3,4},{4,5},{5,6},{6,7},{7,8},{8,9},{9,10},{10,1... | collective-permute-start | bytes 147464 | tf_op jit(solution)/shard_map/ppermute | solution.py:373
  15.0 6.5 %collective-permute-start.3 = (bf16[12,16,128]{2,1,0:T(8,128)(2,1)S(1)}, bf16[12,16,128]{2,1,0:T(8,128)(2,1)S(1)}, u32[]{:S(2)}, u32[]{:S(2)}) collective-permute-start(bf16[12,16,128]{2,1,0:T(8,128)(2,1)S(1)} %get-tuple-element.16), channel_id=1, source_target_pairs={{0,15},{1,0},{2,1},{3,2},{4,3},{5,4},{6,5},{7,6},{8,7},{9,8},{10,9... | collective-permute-start | bytes 147464 | tf_op jit(solution)/shard_map/ppermute | solution.py:373
  38.5 10.0 %all-to-all-start.1 = ((f32[32,8,128]{2,1,0:T(8,128)}), f32[32,8,128]{2,1,0:T(8,128)S(1)}, u32[]{:S(2)}, u32[]{:S(2)}) async-start(f32[32,8,128]{2,1,0:T(8,128)} %lags.2), calls=%async_computation.1 | async-start | bytes 262144 | tf_op jit(solution)/shard_map/all_to_all | solution.py:385

commit v3 on v2

--- a/solution.py
+++ b/solution.py
@@ -57,7 +57,17 @@
     return pltpu.roll(jnp.where(j >= BLK + t, prv, x), -t, x.ndim - 1)
 
 
-def prep_kernel(source, receiver, index, own, south, north):
+def prep_kernel(source_in, receiver_in, index_in, own, south, north, source, receiver, index, sems):
+    copies = [
+        pltpu.make_async_copy(one, two, sems.at[i])
+        for i, (one, two) in enumerate(
+            ((source_in, source), (receiver_in, receiver), (index_in, index))
+        )
+    ]
+    for copy in copies:
+        copy.start()
+    for copy in copies:
+        copy.wait()
     lane = lane_ids((8, LANES))
     planes = (
         (source[0, 0].astype(F32), source[0, 1].astype(F32)),
@@ -65,6 +75,7 @@
         (index[0].astype(F32), index[1].astype(F32)),
     )
     for p, (one, two) in enumerate(planes):
+        classes = []
         for group in range(ROWS // 8):
             rows = slice(8 * group, 8 * group + 8)
             blocks = []
@@ -73,16 +84,18 @@
                 v = two[rows, LANES * g : LANES * g + LANES]
                 blocks.append(jnp.where(lane < BLK, u, swap_halves(v)))
                 blocks.append(jnp.where(lane < BLK, swap_halves(u), v))
-            turned = jnp.swapaxes(jnp.stack(blocks), 0, 1).astype(BF16)
+            turned = jnp.swapaxes(jnp.stack(blocks), 0, 1)
             subs = slice(8 * p, 8 * p + 8)
-            own[rows, subs, :] = turned
+            own[rows, subs, :] = turned.astype(BF16)
             if p < 2:
-                south[rows, subs, :] = turned
-                north[rows, subs, :] = turned
-            else:
-                dest, base = (north, 0) if group == 0 else (south, 4)
-                for i in range(OHALF):
-                    dest[ROWS + i // 2, 8 * (i % 2) : 8 * (i % 2) + 8, :] = turned[base + i]
+                south[rows, subs, :] = turned.astype(BF16)
+                north[rows, subs, :] = turned.astype(BF16)
+            classes += [turned[i] for i in range(8)]
+        if p == 2:
+            for i in range(OHALF):
+                at = (ROWS + i // 2, slice(8 * (i % 2), 8 * (i % 2) + 8))
+                north[at] = classes[i].astype(BF16)
+                south[at] = classes[ROWS - OHALF + i].astype(BF16)
 
 
 def in_vmem(*arrays):
@@ -94,18 +107,28 @@
 SSPEC = pl.BlockSpec(memory_space=pltpu.SMEM)
 
 
+HBM = pl.BlockSpec(memory_space=pltpu.HBM)
+
+
 def prep(source, receiver, index):
     send = pltpu.VMEM((ROWS + 2, 16, LANES), BF16)
     return pl.pallas_call(
         prep_kernel,
         out_shape=(pltpu.VMEM((ROWS, 24, LANES), BF16), send, send),
+        in_specs=[HBM] * 3,
         out_specs=(VSPEC, VSPEC, VSPEC),
+        scratch_shapes=[
+            pltpu.VMEM(source.shape, BF16),
+            pltpu.VMEM(receiver.shape, BF16),
+            pltpu.VMEM(index.shape, jnp.int32),
+            pltpu.SemaphoreType.DMA((3,)),
+        ],
         compiler_params=PARAMS,
         name="prep",
-    )(source, receiver, index)
-
-
-def matrix_kernel(filters, out, base):
+    )(*[pltpu.with_memory_space_constraint(x, pltpu.HBM) for x in (source, receiver, index)])
+
+
+def matrix_kernel(filters, taps, out, splats, base):
     tap = lax.broadcasted_iota(jnp.int32, (FILT, LANES), 0)
     col = lane_ids((FILT, LANES)) % BLK
     perm = ((HALF - tap) % BLK == col).astype(BF16)
@@ -145,17 +168,23 @@
 
     for a in range(FILT):
         one_tap(a)
-
-
-def filter_matrix(filters):
+    for a in range(OFILT):
+        for b in range(OFILT):
+            splats[OFILT * a + b] = jnp.broadcast_to(taps[a, 0:1, b : b + 1], (NB, LANES))
+
+
+def filter_matrix(filters, taps):
     return pl.pallas_call(
         matrix_kernel,
-        out_shape=pltpu.VMEM((FILT, 2 * LANES, 2 * LANES), BF16),
-        out_specs=VSPEC,
+        out_shape=(
+            pltpu.VMEM((FILT, 2 * LANES, 2 * LANES), BF16),
+            pltpu.VMEM((OFILT * OFILT, NB, LANES), F32),
+        ),
+        out_specs=(VSPEC, VSPEC),
         scratch_shapes=[pltpu.VMEM((2 * NV, 32, LANES), F32)],
         compiler_params=PARAMS,
         name="matrix",
-    )(filters)
+    )(filters, taps)
 
 
 def place_rows(buffer, start, rows):
@@ -188,36 +217,41 @@
         if 0 <= i < ROWS:
             both = own[i, 16:24, :].astype(F32)
         else:
-            i = x % ROWS
-            pack = up if x < OHALF else down
-            i = i % OHALF
+            pack, i = (up, x) if x < OHALF else (down, i - ROWS)
             both = pack[ROWS + i // 2, 8 * (i % 2) : 8 * (i % 2) + 8, :].astype(F32)
         swapped = swap_halves(both)
-        mask = jnp.where(lane < BLK, both, swapped) if depth == 0 else jnp.where(lane < BLK, swapped, both)
+        if depth == 0:
+            mask = jnp.where(lane < BLK, both, swapped)
+        else:
+            mask = jnp.where(lane < BLK, swapped, both)
         mask = jnp.concatenate([mask, mask], axis=0)
-        q = jnp.where(mask == 0.0, acc[x, :, :LANES], acc[x, :, LANES:])
+        both = acc[x // HALF][x % HALF]
+        q = jnp.where(mask == 0.0, both[:, :LANES], both[:, LANES:])
         if x < OHALF:
             q = jnp.where(here > 0, q, 0.0)
         if x >= OHALF + ROWS:
             q = jnp.where(here < last, q, 0.0)
-        rows.append(q.astype(BF16))
+        rows.append(q)
     return rows
 
 
-def first_kernel(own, up, down, matrix, lines, south, north, top):
+def place_sides(buffer, up, down, n, middle):
     here = lax.axis_index("row")
     last = lax.axis_size("row") - 1
-    place_rows(top, 0, jnp.where(here > 0, up[0:ROWS].astype(F32), 0.0))
+    place_rows(buffer, 0, jnp.where(here > 0, up[0:n].astype(F32), 0.0))
+    place_rows(buffer, n + middle, jnp.where(here < last, down[0:n].astype(F32), 0.0))
+
+
+def first_kernel(own, up, down, matrix, lines, south, north, top):
     place_rows(top, ROWS, own[:, 0:16, :].astype(F32))
-    place_rows(top, 2 * ROWS, jnp.where(here < last, down[0:ROWS].astype(F32), 0.0))
-    rows = pick(filter_rows(top, matrix), own, up, down, 0)
+    place_sides(top, up, down, ROWS, ROWS)
+    acc = filter_rows(top, matrix)
+    rows = pick((acc[0:HALF], acc[HALF:EXT]), own, up, down, 0)
     for x, q in enumerate(rows):
-        lines[x] = q
-        i = x - OHALF
-        if 0 <= i < HALF:
-            north[i] = q
-        if ROWS - HALF <= i < ROWS:
-            south[i - OHALF] = q
+        lines[x] = q.astype(BF16)
+    for i in range(HALF):
+        south[i] = rows[OHALF + i].astype(BF16)
+        north[i] = rows[2 * OHALF + i].astype(BF16)
 
 
 def first_step(own, up, down, matrix):
@@ -233,28 +267,64 @@
     )(*in_vmem(own, up, down, matrix))
 
 
-def second_kernel(own, up, down, matrix, done, above, below, lines, mid):
+def inner_kernel(done, matrix, acc, lines, mid):
+    zero = jnp.zeros((HALF, 16, 2 * LANES), BF16)
+    mid[0:HALF] = zero
+    mid[HALF + EXT :] = zero
+    place_rows(mid, HALF, done[...].astype(F32))
+    acc[...] = filter_rows(mid, matrix)
+    lines[...] = done[...]
+
+
+def inner_step(done, matrix):
+    return pl.pallas_call(
+        inner_kernel,
+        out_shape=(
+            pltpu.VMEM((EXT, 16, 2 * LANES), F32),
+            pltpu.VMEM((EXT, 16, LANES), BF16),
+        ),
+        in_specs=[VSPEC] * 2,
+        out_specs=(VSPEC, VSPEC),
+        scratch_shapes=[pltpu.VMEM((MID, 16, 2 * LANES), BF16)],
+        compiler_params=PARAMS,
+        name="inner",
+    )(*in_vmem(done, matrix))
+
+
+def outer_kernel(own, up, down, matrix, part, done, above, below, lines, high, low):
+    zero = jnp.zeros((HALF, 16, 2 * LANES), BF16)
     here = lax.axis_index("row")
     last = lax.axis_size("row") - 1
-    place_rows(mid, 0, jnp.where(here > 0, above[...].astype(F32), 0.0))
-    place_rows(mid, HALF, done[...].astype(F32))
-    place_rows(mid, HALF + EXT, jnp.where(here < last, below[...].astype(F32), 0.0))
+    place_rows(high, 0, jnp.where(here > 0, above[...].astype(F32), 0.0))
+    high[HALF:] = zero
+    low[0:HALF] = zero
+    place_rows(low, HALF, jnp.where(here < last, below[...].astype(F32), 0.0))
     lines[0:EXT] = done[...]
-    rows = pick(filter_rows(mid, matrix), own, up, down, 1)
-    for x, q in enumerate(rows):
-        lines[EXT + x] = q
-
-
-def second_step(own, up, down, matrix, done, above, below):
-    return pl.pallas_call(
-        second_kernel,
+
+    def edge(buffer, shift, taps):
+        acc = None
+        for a in taps:
+            layer = buffer[a - shift : a - shift + HALF].reshape(HALF * 16, 2 * LANES)
+            term = jnp.dot(layer, matrix[a], preferred_element_type=F32)
+            acc = term if acc is None else acc + term
+        return acc.reshape(HALF, 16, 2 * LANES)
+
+    top = part[0:HALF] + edge(high, 0, range(HALF))
+    bottom = part[HALF:EXT] + edge(low, HALF, range(HALF + 1, FILT))
+    for x, q in enumerate(pick((top, bottom), own, up, down, 1)):
+        lines[EXT + x] = q.astype(BF16)
+
+
+def outer_step(own, up, down, matrix, part, done, above, below):
+    return pl.pallas_call(
+        outer_kernel,
         out_shape=pltpu.VMEM((LINES, 16, LANES), BF16),
-        in_specs=[VSPEC] * 7,
+        in_specs=[VSPEC] * 8,
         out_specs=VSPEC,
-        scratch_shapes=[pltpu.VMEM((MID, 16, 2 * LANES), BF16)],
-        compiler_params=PARAMS,
-        name="second",
-    )(*in_vmem(own, up, down, matrix, done, above, below))
+        scratch_shapes=[pltpu.VMEM((EXT, 16, 2 * LANES), BF16)] * 2,
+        compiler_params=PARAMS,
+        name="outer",
+    )(*in_vmem(own, up, down, matrix, part, done, above, below))
 
 
 def shift_table():
@@ -317,7 +387,7 @@
     )(lags, *in_vmem(fields, table))
 
 
-def image_kernel(taps, raw, out, rows, nxt, prv):
+def image_kernel(splats, raw, out, rows, nxt, prv, image, sems):
     lane = lane_ids((NB, LANES))
 
     def piece(depth, x, high):
@@ -334,6 +404,7 @@
         flipped = swap_halves(v)
         nxt[x] = next_block(flipped)
         prv[x] = prev_block(flipped)
+    copies = []
     for group in range(ROWS // 8):
         accs = [None] * 8
         for b in range(OFILT):
@@ -342,28 +413,40 @@
                 for x in range(8 + 2 * OHALF)
             ]
             for a in range(OFILT):
-                w = taps[0, a, b]
+                w = splats[OFILT * a + b]
                 for x in range(8):
                     term = moved[x + a] * w
                     accs[x] = term if accs[x] is None else accs[x] + term
         z = jnp.swapaxes(jnp.stack(accs), 0, 1)
-        rows8 = slice(8 * group, 8 * group + 8)
         for g in range(WIDTH // LANES):
             even, odd = z[2 * g], z[2 * g + 1]
             cols = slice(LANES * g, LANES * g + LANES)
-            out[0, 0, rows8, cols] = jnp.where(lane < BLK, even, swap_halves(odd))
-            out[1, 0, rows8, cols] = jnp.where(lane < BLK, swap_halves(even), odd)
-
-
-def filter_image(taps, raw):
+            image[group, 0, 0, :, cols] = jnp.where(lane < BLK, even, swap_halves(odd))
+            image[group, 1, 0, :, cols] = jnp.where(lane < BLK, swap_halves(even), odd)
+
+        copy = pltpu.make_async_copy(
+            image.at[group], out.at[:, :, pl.ds(8 * group, 8), :], sems.at[group]
+        )
+        copy.start()
+        copies.append(copy)
+    for copy in copies:
+        copy.wait()
+
+
+def filter_image(splats, raw):
     return pl.pallas_call(
         image_kernel,
         out_shape=jax.ShapeDtypeStruct((DEPTHS, 1, ROWS, WIDTH), F32),
-        in_specs=[SSPEC, VSPEC],
-        scratch_shapes=[pltpu.VMEM((EXT, NB, LANES), F32)] * 3,
+        in_specs=[VSPEC, VSPEC],
+        out_specs=HBM,
+        scratch_shapes=[pltpu.VMEM((EXT, NB, LANES), F32)] * 3
+        + [
+            pltpu.VMEM((ROWS // 8, DEPTHS, 1, 8, WIDTH), F32),
+            pltpu.SemaphoreType.DMA((ROWS // 8,)),
+        ],
         compiler_params=PARAMS,
         name="image",
-    )(taps, *in_vmem(raw))
+    )(*in_vmem(splats, raw))
 
 
 def body(source, receiver, filters, table_index, lags, offset_filters):
@@ -375,15 +458,16 @@
     own, south, north = prep(source, receiver, table_index)
     up = shifted(south, 1)
     down = shifted(north, -1)
-    matrix = filter_matrix(filters)
+    matrix, splats = filter_matrix(filters, jnp.transpose(offset_filters, (1, 0, 2)))
     done, south, north = first_step(own, up, down, matrix)
-    above = shifted(north, 1)
-    below = shifted(south, -1)
-    lines = second_step(own, up, down, matrix, done, above, below)
+    above = shifted(south, 1)
+    below = shifted(north, -1)
+    part, done = inner_step(done, matrix)
+    lines = outer_step(own, up, down, matrix, part, done, above, below)
     fields = lax.all_to_all(lines, "freq", 0, 0, tiled=True)
     raw = gather_lags(lags, fields)
     raw = lax.all_to_all(raw, "freq", 0, 0, tiled=True)
-    return filter_image(offset_filters, raw)
+    return filter_image(splats, raw)
 
 
 def solution(mesh):

time: 50.8 us -> 46.6 us (0.917)
  blocking collectives: 13.5 us -> 22 us
  waiting for transfers between devices: 7.51 us -> 0.02 us
  starting transfers between devices: 18.3 us -> 14.3 us
  local copies, waits for them, and re-layouts: 3.12 us -> 1.44 us
  Pallas kernels: 7.88 us -> 8.4 us
    all_to_all x0 -> x1, blocking collectives: none -> 9.07 us  [body(): raw = lax.all_to_all(raw, 'freq', 0, 0, tiled=True)]
    all_to_all x1 -> x0, waiting for transfers between devices: 6.11 us -> none  [body(): raw = lax.all_to_all(raw, 'freq', 0, 0, tiled=True)]
    all_to_all x1 -> x0, starting transfers between devices: 3.84 us -> none  [body(): raw = lax.all_to_all(raw, 'freq', 0, 0, tiled=True)]
    unnamed x14 -> x7, local copies, waits for them, and re-layouts: 3.12 us -> 1.44 us
    ppermute x4, waiting for transfers between devices: 1.4 us -> 0.02 us  [shifted(): lax.ppermute(x, 'row', [(i, (i + step) % count) for i in range(count)])]
    pallas_call x2 -> x3, Pallas kernels: 2.4 us -> 3.32 us  [the longest x1 1.45 us: inner_step(): pl.pallas_call(inner_kernel, out_shape=(pltpu.VMEM((EXT, 16, 2 * LANES),...]
    pallas_call x1, Pallas kernels: 0.13 us -> 1.03 us  [prep(): pl.pallas_call(prep_kernel, out_shape=(pltpu.VMEM((ROWS, 24, LANES), BF16...]
    pallas_call x1, Pallas kernels: 1.96 us -> 1.3 us  [filter_image(): pl.pallas_call(image_kernel, out_shape=jax.ShapeDtypeStruct((DEPTHS, 1, R...]
  transfers between devices with their start and end apart: 5 -> 4, of which waited for: 2 -> 0; matrix products, arithmetic and copies ran while one was open for 1% -> 2% of each run, Pallas kernels for 2% -> 5%
where the time goes in v3:
time: 46.6 us; the launch traced here: 46.3 us
  blocking collectives  22 us (47%)
  starting transfers between devices  14.3 us (31%)
  Pallas kernels  8.4 us (18%)
  local copies, waits for them, and re-layouts  1.44 us (3%)
    ppermute x4, starting transfers between devices, shifted(): lax.ppermute(x, 'row', [(i, (i + step) % count) for i in range(count)])  14.3 us
    all_to_all x1, blocking collectives, body(): fields = lax.all_to_all(lines, 'freq', 0, 0, tiled=True)  12.9 us
    all_to_all x1, blocking collectives, body(): raw = lax.all_to_all(raw, 'freq', 0, 0, tiled=True)  9.07 us
    pallas_call x1, Pallas kernels, first_step(): pl.pallas_call(first_kernel, out_shape=(pltpu.VMEM((EXT, 16, LANES), BF16...  1.45 us
    pallas_call x1, Pallas kernels, inner_step(): pl.pallas_call(inner_kernel, out_shape=(pltpu.VMEM((EXT, 16, 2 * LANES),...  1.45 us
    unnamed x7, local copies, waits for them, and re-layouts  1.44 us
    pallas_call x1, Pallas kernels, filter_image(): pl.pallas_call(image_kernel, out_shape=jax.ShapeDtypeStruct((DEPTHS, 1, R...  1.3 us
    pallas_call x1, Pallas kernels, gather_lags(): pl.pallas_call(gather_kernel, out_shape=pltpu.VMEM((2 * NOFF, NB, LANES),...  1.29 us
  transfers between devices with their start and end apart: 4, of which 0 were waited for; matrix products, arithmetic and copies ran while one was open for 2% of the time, Pallas kernels for 5%

profile of v3, /device:TPU:1, one launch (start us, length us, event | category | flops | bytes accessed | tf_op | source)
XLA Modules:
  0.0 46.3 jit_solution(10441142616530039238)
XLA Ops:
  0.0 1.0 %prep.1 = (bf16[16,24,128]{2,1,0:T(8,128)(2,1)S(1)}, bf16[18,16,128]{2,1,0:T(8,128)(2,1)S(1)}, bf16[18,16,128]{2,1,0:T(8,128)(2,1)S(1)}) custom-call(bf16[1,2,16,512]{3,2,1,0:T(8,128)(2,1)} %source_in.1, bf16[1,2,16,512]{3,2,1,0:T(8,128)(2,1)} %receiver_in.1, s32[2,16,512]{2,1,0:T(8,128)} %index_in.1), custom_call_target="tpu_custom_call" | custom-call | tf_op jit(solution)/shard_map/prep/pallas_call | solution.py:115
  1.0 2.5 %collective-permute-start = (bf16[18,16,128]{2,1,0:T(8,128)(2,1)S(1)}, bf16[18,16,128]{2,1,0:T(8,128)(2,1)S(1)}, u32[]{:S(2)}, u32[]{:S(2)}) collective-permute-start(bf16[18,16,128]{2,1,0:T(8,128)(2,1)S(1)} %get-tuple-element.17), channel_id=1, source_target_pairs={{0,1},{1,2},{2,3},{3,4},{4,5},{5,6},{6,7},{7,8},{8,9},{9,10},{10,1... | collective-permute-start | bytes 221192 | tf_op jit(solution)/shard_map/ppermute | solution.py:456
  3.6 6.7 %collective-permute-start.1 = (bf16[18,16,128]{2,1,0:T(8,128)(2,1)S(1)}, bf16[18,16,128]{2,1,0:T(8,128)(2,1)S(1)}, u32[]{:S(2)}, u32[]{:S(2)}) collective-permute-start(bf16[18,16,128]{2,1,0:T(8,128)(2,1)S(1)} %get-tuple-element.18), channel_id=1, source_target_pairs={{0,15},{1,0},{2,1},{3,2},{4,3},{5,4},{6,5},{7,6},{8,7},{9,8},{10,9... | collective-permute-start | bytes 221192 | tf_op jit(solution)/shard_map/ppermute | solution.py:456
  10.2 0.7 %copy.8.filters = bf16[1,2,2,25,25]{4,3,2,1,0:T(8,128)(2,1)S(1)} copy(bf16[1,2,2,25,25]{4,2,3,1,0:T(2,128)(2,1)} %param.9) | data formatting | bytes 10000 | tf_op args[2]
  11.0 0.0 copy-start.1
  11.0 0.7 %copy-done.1 = f32[1,9,9]{2,0,1:T(1,128)S(1)} copy-done((f32[1,9,9]{2,0,1:T(1,128)S(1)}, f32[1,9,9]{2,0,1:T(1,128)}, u32[]{:S(2)}) %copy-start.1) | copy-done | bytes 348
  11.7 1.1 %matrix.1 = (bf16[25,256,256]{2,1,0:T(8,128)(2,1)S(1)}, f32[81,8,128]{2,1,0:T(8,128)S(1)}) custom-call(bf16[1,2,2,25,25]{4,3,2,1,0:T(8,128)(2,1)S(1)} %copy.8.filters, f32[9,1,9]{2,1,0:T(1,128)S(1)} %bitcast.1), custom_call_target="tpu_custom_call" | custom-call | tf_op jit(solution)/shard_map/matrix/pallas_call | solution.py:177
  12.8 0.0 collective-permute-done.up
  12.8 0.0 collective-permute-done.1.down
  12.8 1.4 %first.1 = (bf16[24,16,128]{2,1,0:T(8,128)(2,1)S(1)}, bf16[12,16,128]{2,1,0:T(8,128)(2,1)S(1)}, bf16[12,16,128]{2,1,0:T(8,128)(2,1)S(1)}) custom-call(bf16[16,24,128]{2,1,0:T(8,128)(2,1)S(1)} %get-tuple-element.16.own, bf16[18,16,128]{2,1,0:T(8,128)(2,1)S(1)} %collective-permute-done.up, bf16[18,16,128]{2,1,0:T(8,128)(2,1)S(1)} %collective-permute-done.1.down, ...), custom_call_target="tpu_custom_call" | custom-call | tf_op jit(solution)/shard_map/first/pallas_call | solution.py:259
  14.2 0.1 collective-permute-start.2
  14.3 5.1 %collective-permute-start.3 = (bf16[12,16,128]{2,1,0:T(8,128)(2,1)S(1)}, bf16[12,16,128]{2,1,0:T(8,128)(2,1)S(1)}, u32[]{:S(2)}, u32[]{:S(2)}) collective-permute-start(bf16[12,16,128]{2,1,0:T(8,128)(2,1)S(1)} %get-tuple-element.24), channel_id=1, source_target_pairs={{0,15},{1,0},{2,1},{3,2},{4,3},{5,4},{6,5},{7,6},{8,7},{9,8},{10,9... | collective-permute-start | bytes 147464 | tf_op jit(solution)/shard_map/ppermute | solution.py:456
  19.4 0.0 copy-start
  19.4 0.0 copy-start.2
  19.4 1.4 %inner.1 = (f32[24,16,256]{2,1,0:T(8,128)S(1)}, bf16[24,16,128]{2,1,0:T(8,128)(2,1)S(1)}) custom-call(bf16[24,16,128]{2,1,0:T(8,128)(2,1)S(1)} %get-tuple-element.20.done, bf16[25,256,256]{2,1,0:T(8,128)(2,1)S(1)} %get-tuple-element.19.matrix), custom_call_target="tpu_custom_call" | custom-call | tf_op jit(solution)/shard_map/inner/pallas_call | solution.py:280
  20.8 0.0 collective-permute-done.2.above
  20.9 0.0 collective-permute-done.3.below
  20.9 0.8 %outer.1 = bf16[48,16,128]{2,1,0:T(8,128)(2,1)S(1)} custom-call(bf16[16,24,128]{2,1,0:T(8,128)(2,1)S(1)} %get-tuple-element.16.own, bf16[18,16,128]{2,1,0:T(8,128)(2,1)S(1)} %collective-permute-done.up, bf16[18,16,128]{2,1,0:T(8,128)(2,1)S(1)} %collective-permute-done.1.down, bf16[25,256,256]{2,1,0:T(8,128)(2,1)S(1)} %get-tuple-element.19.matrix, ...), custom_call_target="tpu_custom_call" | custom-call | tf_op jit(solution)/shard_map/outer/pallas_call | solution.py:319
  21.7 12.9 %all_to_all.10.fields = bf16[48,16,128]{2,1,0:T(8,128)(2,1)S(1)} all-to-all(bf16[48,16,128]{2,1,0:T(8,128)(2,1)S(1)} %outer.1), channel_id=1, replica_groups=mesh['freq'=16,'row'=16] {'freq'}, dimensions={0} | all-to-all | bytes 393216 | tf_op jit(solution)/shard_map/all_to_all | solution.py:467
  34.6 0.0 copy-done
  34.6 0.0 copy-done.2
  34.6 1.3 %lags.2 = f32[32,8,128]{2,1,0:T(8,128)S(1)} custom-call(s32[16]{0:T(128)S(1)} %copy-done.2, bf16[48,16,128]{2,1,0:T(8,128)(2,1)S(1)} %all_to_all.10.fields, bf16[256,2048]{1,0:T(8,128)(2,1)S(1)} %copy-done), custom_call_target="tpu_custom_call" | custom-call | tf_op jit(solution)/shard_map/lags/pallas_call | solution.py:375
  35.9 9.1 %all_to_all.11.raw = f32[32,8,128]{2,1,0:T(8,128)S(1)} all-to-all(f32[32,8,128]{2,1,0:T(8,128)S(1)} %lags.2), channel_id=1, replica_groups=mesh['freq'=16,'row'=16] {'freq'}, dimensions={0} | all-to-all | bytes 262144 | tf_op jit(solution)/shard_map/all_to_all | solution.py:469
  45.0 1.3 %image.1 = f32[2,1,16,512]{3,2,1,0:T(8,128)} custom-call(f32[81,8,128]{2,1,0:T(8,128)S(1)} %get-tuple-element.15.splats, f32[32,8,128]{2,1,0:T(8,128)S(1)} %all_to_all.11.raw), custom_call_target="tpu_custom_call" | custom-call | tf_op jit(solution)/shard_map/image/pallas_call | solution.py:437
Async XLA Ops:
  1.0 11.7 %collective-permute-start = (bf16[18,16,128]{2,1,0:T(8,128)(2,1)S(1)}, bf16[18,16,128]{2,1,0:T(8,128)(2,1)S(1)}, u32[]{:S(2)}, u32[]{:S(2)}) collective-permute-start(bf16[18,16,128]{2,1,0:T(8,128)(2,1)S(1)} %get-tuple-element.17), channel_id=1, source_target_pairs={{0,1},{1,2},{2,3},{3,4},{4,5},{5,6},{6,7},{7,8},{8,9},{9,10},{10,1... | collective-permute-start | bytes 221192 | tf_op jit(solution)/shard_map/ppermute | solution.py:456
  3.6 9.2 %collective-permute-start.1 = (bf16[18,16,128]{2,1,0:T(8,128)(2,1)S(1)}, bf16[18,16,128]{2,1,0:T(8,128)(2,1)S(1)}, u32[]{:S(2)}, u32[]{:S(2)}) collective-permute-start(bf16[18,16,128]{2,1,0:T(8,128)(2,1)S(1)} %get-tuple-element.18), channel_id=1, source_target_pairs={{0,15},{1,0},{2,1},{3,2},{4,3},{5,4},{6,5},{7,6},{8,7},{9,8},{10,9... | collective-permute-start | bytes 221192 | tf_op jit(solution)/shard_map/ppermute | solution.py:456
  11.0 0.7 %copy-start.1 = (f32[1,9,9]{2,0,1:T(1,128)S(1)}, f32[1,9,9]{2,0,1:T(1,128)}, u32[]{:S(2)}) copy-start(f32[1,9,9]{2,0,1:T(1,128)} %param.12) | copy-start | bytes 976
  14.2 6.6 %collective-permute-start.2 = (bf16[12,16,128]{2,1,0:T(8,128)(2,1)S(1)}, bf16[12,16,128]{2,1,0:T(8,128)(2,1)S(1)}, u32[]{:S(2)}, u32[]{:S(2)}) collective-permute-start(bf16[12,16,128]{2,1,0:T(8,128)(2,1)S(1)} %get-tuple-element.23), channel_id=1, source_target_pairs={{0,1},{1,2},{2,3},{3,4},{4,5},{5,6},{6,7},{7,8},{8,9},{9,10},{10,1... | collective-permute-start | bytes 147464 | tf_op jit(solution)/shard_map/ppermute | solution.py:456
  14.3 6.5 %collective-permute-start.3 = (bf16[12,16,128]{2,1,0:T(8,128)(2,1)S(1)}, bf16[12,16,128]{2,1,0:T(8,128)(2,1)S(1)}, u32[]{:S(2)}, u32[]{:S(2)}) collective-permute-start(bf16[12,16,128]{2,1,0:T(8,128)(2,1)S(1)} %get-tuple-element.24), channel_id=1, source_target_pairs={{0,15},{1,0},{2,1},{3,2},{4,3},{5,4},{6,5},{7,6},{8,7},{9,8},{10,9... | collective-permute-start | bytes 147464 | tf_op jit(solution)/shard_map/ppermute | solution.py:456
  19.4 15.2 %copy-start = (bf16[256,2048]{1,0:T(8,128)(2,1)S(1)}, bf16[256,2048]{1,0:T(8,128)(2,1)}, u32[]{:S(2)}) copy-start(bf16[256,2048]{1,0:T(8,128)(2,1)} %constant.2.clone.table) | copy-start | bytes 3145732
  19.4 15.2 %copy-start.2 = (s32[16]{0:T(128)S(1)}, s32[16]{0:T(128)}, u32[]{:S(2)}) copy-start(s32[16]{0:T(128)} %lags.3) | copy-start | bytes 196

commit v4 on v3

--- a/solution.py
+++ b/solution.py
@@ -57,11 +57,21 @@
     return pltpu.roll(jnp.where(j >= BLK + t, prv, x), -t, x.ndim - 1)
 
 
-def prep_kernel(source_in, receiver_in, index_in, own, south, north, source, receiver, index, sems):
+def prep_kernel(
+    source_in, receiver_in, index_in, filters_in, taps_in,
+    own, south, north, filters, taps,
+    source, receiver, index, sems,
+):
     copies = [
         pltpu.make_async_copy(one, two, sems.at[i])
         for i, (one, two) in enumerate(
-            ((source_in, source), (receiver_in, receiver), (index_in, index))
+            (
+                (source_in, source),
+                (receiver_in, receiver),
+                (index_in, index),
+                (filters_in, filters),
+                (taps_in, taps),
+            )
         )
     ]
     for copy in copies:
@@ -110,33 +120,41 @@
 HBM = pl.BlockSpec(memory_space=pltpu.HBM)
 
 
-def prep(source, receiver, index):
+def prep(*args):
+    source, receiver, index, filters, taps = args
     send = pltpu.VMEM((ROWS + 2, 16, LANES), BF16)
     return pl.pallas_call(
         prep_kernel,
-        out_shape=(pltpu.VMEM((ROWS, 24, LANES), BF16), send, send),
-        in_specs=[HBM] * 3,
-        out_specs=(VSPEC, VSPEC, VSPEC),
+        out_shape=(
+            pltpu.VMEM((ROWS, 24, LANES), BF16),
+            send,
+            send,
+            pltpu.VMEM(filters.shape, BF16),
+            pltpu.VMEM(taps.shape, F32),
+        ),
+        in_specs=[HBM] * 5,
+        out_specs=(VSPEC,) * 5,
         scratch_shapes=[
             pltpu.VMEM(source.shape, BF16),
             pltpu.VMEM(receiver.shape, BF16),
             pltpu.VMEM(index.shape, jnp.int32),
-            pltpu.SemaphoreType.DMA((3,)),
+            pltpu.SemaphoreType.DMA((5,)),
         ],
         compiler_params=PARAMS,
         name="prep",
-    )(*[pltpu.with_memory_space_constraint(x, pltpu.HBM) for x in (source, receiver, index)])
-
-
-def matrix_kernel(filters, taps, out, splats, base):
+    )(*[pltpu.with_memory_space_constraint(x, pltpu.HBM) for x in args])
+
+
+def matrix_kernel(filters, taps, out, splats, flat, base):
     tap = lax.broadcasted_iota(jnp.int32, (FILT, LANES), 0)
     col = lane_ids((FILT, LANES)) % BLK
     perm = ((HALF - tap) % BLK == col).astype(BF16)
     for v in range(NV):
-        for part in range(2):
-            base[2 * v + part, 0:FILT, :] = jnp.dot(
-                filters[0, v, part], perm, preferred_element_type=F32
-            )
+        for a in range(FILT):
+            flat[v, 2 * a : 2 * a + 2, 0:FILT] = filters[0, v, a].astype(F32)
+        base[v] = jnp.dot(
+            flat[v, 0 : 2 * FILT, 0:FILT].astype(BF16), perm, preferred_element_type=F32
+        )
     lane = lane_ids((16, LANES))
     row = lax.broadcasted_iota(jnp.int32, (16, LANES), 0)
     zero = jnp.zeros((16, LANES), BF16)
@@ -145,7 +163,7 @@
         for v in range(NV):
             turned = []
             for part in range(2):
-                taps = jnp.broadcast_to(base[2 * v + part, pl.ds(a, 1), :], (BLK, LANES))
+                taps = jnp.broadcast_to(base[v, 2 * a + part : 2 * a + part + 1, :], (BLK, LANES))
                 turned.append(pltpu.roll(taps, 0, 1, stride=1, stride_axis=0))
             cols = slice(v * LANES, v * LANES + LANES)
             for top in range(0, BLK, 16):
@@ -181,10 +199,13 @@
             pltpu.VMEM((OFILT * OFILT, NB, LANES), F32),
         ),
         out_specs=(VSPEC, VSPEC),
-        scratch_shapes=[pltpu.VMEM((2 * NV, 32, LANES), F32)],
+        scratch_shapes=[
+            pltpu.VMEM((NV, 56, LANES), F32),
+            pltpu.VMEM((NV, 2 * FILT, LANES), F32),
+        ],
         compiler_params=PARAMS,
         name="matrix",
-    )(filters, taps)
+    )(*in_vmem(filters, taps))
 
 
 def place_rows(buffer, start, rows):
@@ -455,10 +476,16 @@
     def shifted(x, step):
         return lax.ppermute(x, "row", [(i, (i + step) % count) for i in range(count)])
 
-    own, south, north = prep(source, receiver, table_index)
+    own, south, north, filters, taps = prep(
+        source,
+        receiver,
+        table_index,
+        jnp.transpose(filters, (0, 1, 3, 2, 4)),
+        jnp.transpose(offset_filters, (1, 0, 2)),
+    )
     up = shifted(south, 1)
     down = shifted(north, -1)
-    matrix, splats = filter_matrix(filters, jnp.transpose(offset_filters, (1, 0, 2)))
+    matrix, splats = filter_matrix(filters, taps)
     done, south, north = first_step(own, up, down, matrix)
     above = shifted(south, 1)
     below = shifted(north, -1)

time: 46.6 us -> 46.3 us (level)
  local copies, waits for them, and re-layouts: 1.44 us -> 0.01 us
  waiting for transfers between devices: 0.02 us -> 0.57 us
  blocking collectives: 22 us -> 22.5 us
    unnamed x7 -> x4, local copies, waits for them, and re-layouts: 1.44 us -> 0.01 us
    ppermute x4, waiting for transfers between devices: 0.02 us -> 0.57 us  [shifted(): lax.ppermute(x, 'row', [(i, (i + step) % count) for i in range(count)])]
    all_to_all x1, blocking collectives: 12.9 us -> 13.5 us  [body(): fields = lax.all_to_all(lines, 'freq', 0, 0, tiled=True)]
  transfers between devices with their start and end apart: 4 -> 4, of which waited for: 0 -> 1; matrix products, arithmetic and copies ran while one was open for 2% -> 0% of each run, Pallas kernels for 5% -> 5%
where the time goes in v4:
time: 46.3 us; the launch traced here: 46.1 us
  blocking collectives  22.5 us (49%)
  starting transfers between devices  14.5 us (31%)
  Pallas kernels  8.43 us (18%)
  waiting for transfers between devices  0.57 us (1%)
    ppermute x4, starting transfers between devices, shifted(): lax.ppermute(x, 'row', [(i, (i + step) % count) for i in range(count)])  14.5 us
    all_to_all x1, blocking collectives, body(): fields = lax.all_to_all(lines, 'freq', 0, 0, tiled=True)  13.5 us
    all_to_all x1, blocking collectives, body(): raw = lax.all_to_all(raw, 'freq', 0, 0, tiled=True)  9.06 us
    pallas_call x1, Pallas kernels, first_step(): pl.pallas_call(first_kernel, out_shape=(pltpu.VMEM((EXT, 16, LANES), BF16...  1.45 us
    pallas_call x1, Pallas kernels, inner_step(): pl.pallas_call(inner_kernel, out_shape=(pltpu.VMEM((EXT, 16, 2 * LANES),...  1.44 us
    pallas_call x1, Pallas kernels, gather_lags(): pl.pallas_call(gather_kernel, out_shape=pltpu.VMEM((2 * NOFF, NB, LANES),...  1.3 us
    pallas_call x1, Pallas kernels, filter_image(): pl.pallas_call(image_kernel, out_shape=jax.ShapeDtypeStruct((DEPTHS, 1, R...  1.3 us
    pallas_call x1, Pallas kernels, filter_matrix(): pl.pallas_call(matrix_kernel, out_shape=(pltpu.VMEM((FILT, 2 * LANES, 2 *...  1.09 us
  transfers between devices with their start and end apart: 4, of which 1 were waited for; matrix products, arithmetic and copies ran while one was open for 0% of the time, Pallas kernels for 5%

profile of v4, /device:TPU:1, one launch (start us, length us, event | category | flops | bytes accessed | tf_op | source)
XLA Modules:
  0.0 46.1 jit_solution(14337196873567537630)
XLA Ops:
  0.0 1.1 %prep.1 = (bf16[16,24,128]{2,1,0:T(8,128)(2,1)S(1)}, bf16[18,16,128]{2,1,0:T(8,128)(2,1)S(1)}, bf16[18,16,128]{2,1,0:T(8,128)(2,1)S(1)}, bf16[1,2,25,2,25]{4,3,2,1,0:T(2,128)(2,1)S(1)}, f32[9,1,9]{2,1,0:T(1,128)S(1)}) custom-call(bf16[1,2,16,512]{3,2,1,0:T(8,128)(2,1)} %source_in.1, bf16[1,2,16,512]{3,2,1,0:T(8,128)(2,1)} %receiver_in.1, ...), custom_call_target="tpu_custom_call" | custom-call | tf_op jit(solution)/shard_map/prep/pallas_call | solution.py:126
  1.1 2.5 %collective-permute-start = (bf16[18,16,128]{2,1,0:T(8,128)(2,1)S(1)}, bf16[18,16,128]{2,1,0:T(8,128)(2,1)S(1)}, u32[]{:S(2)}, u32[]{:S(2)}) collective-permute-start(bf16[18,16,128]{2,1,0:T(8,128)(2,1)S(1)} %get-tuple-element.21), channel_id=1, source_target_pairs={{0,1},{1,2},{2,3},{3,4},{4,5},{5,6},{6,7},{7,8},{8,9},{9,10},{10,1... | collective-permute-start | bytes 221192 | tf_op jit(solution)/shard_map/ppermute | solution.py:477
  3.6 6.7 %collective-permute-start.1 = (bf16[18,16,128]{2,1,0:T(8,128)(2,1)S(1)}, bf16[18,16,128]{2,1,0:T(8,128)(2,1)S(1)}, u32[]{:S(2)}, u32[]{:S(2)}) collective-permute-start(bf16[18,16,128]{2,1,0:T(8,128)(2,1)S(1)} %get-tuple-element.22), channel_id=1, source_target_pairs={{0,15},{1,0},{2,1},{3,2},{4,3},{5,4},{6,5},{7,6},{8,7},{9,8},{10,9... | collective-permute-start | bytes 221192 | tf_op jit(solution)/shard_map/ppermute | solution.py:477
  10.3 1.1 %matrix.1 = (bf16[25,256,256]{2,1,0:T(8,128)(2,1)S(1)}, f32[81,8,128]{2,1,0:T(8,128)S(1)}) custom-call(bf16[1,2,25,2,25]{4,3,2,1,0:T(2,128)(2,1)S(1)} %get-tuple-element.17.filters, f32[9,1,9]{2,1,0:T(1,128)S(1)} %get-tuple-element.18.taps), custom_call_target="tpu_custom_call" | custom-call | tf_op jit(solution)/shard_map/matrix/pallas_call | solution.py:195
  11.3 0.6 %collective-permute-done.up = bf16[18,16,128]{2,1,0:T(8,128)(2,1)S(1)} collective-permute-done((bf16[18,16,128]{2,1,0:T(8,128)(2,1)S(1)}, bf16[18,16,128]{2,1,0:T(8,128)(2,1)S(1)}, u32[]{:S(2)}, u32[]{:S(2)}) %collective-permute-start) | collective-permute-done | bytes 73760 | tf_op jit(solution)/shard_map/ppermute | solution.py:477
  11.9 0.0 collective-permute-done.1.down
  11.9 1.4 %first.1 = (bf16[24,16,128]{2,1,0:T(8,128)(2,1)S(1)}, bf16[12,16,128]{2,1,0:T(8,128)(2,1)S(1)}, bf16[12,16,128]{2,1,0:T(8,128)(2,1)S(1)}) custom-call(bf16[16,24,128]{2,1,0:T(8,128)(2,1)S(1)} %get-tuple-element.20.own, bf16[18,16,128]{2,1,0:T(8,128)(2,1)S(1)} %collective-permute-done.up, bf16[18,16,128]{2,1,0:T(8,128)(2,1)S(1)} %collective-permute-done.1.down, ...), custom_call_target="tpu_custom_call" | custom-call | tf_op jit(solution)/shard_map/first/pallas_call | solution.py:280
  13.4 0.1 collective-permute-start.2
  13.5 5.2 %collective-permute-start.3 = (bf16[12,16,128]{2,1,0:T(8,128)(2,1)S(1)}, bf16[12,16,128]{2,1,0:T(8,128)(2,1)S(1)}, u32[]{:S(2)}, u32[]{:S(2)}) collective-permute-start(bf16[12,16,128]{2,1,0:T(8,128)(2,1)S(1)} %get-tuple-element.28), channel_id=1, source_target_pairs={{0,15},{1,0},{2,1},{3,2},{4,3},{5,4},{6,5},{7,6},{8,7},{9,8},{10,9... | collective-permute-start | bytes 147464 | tf_op jit(solution)/shard_map/ppermute | solution.py:477
  18.7 0.0 copy-start
  18.7 0.0 copy-start.1
  18.7 1.4 %inner.1 = (f32[24,16,256]{2,1,0:T(8,128)S(1)}, bf16[24,16,128]{2,1,0:T(8,128)(2,1)S(1)}) custom-call(bf16[24,16,128]{2,1,0:T(8,128)(2,1)S(1)} %get-tuple-element.24.done, bf16[25,256,256]{2,1,0:T(8,128)(2,1)S(1)} %get-tuple-element.23.matrix), custom_call_target="tpu_custom_call" | custom-call | tf_op jit(solution)/shard_map/inner/pallas_call | solution.py:301
  20.1 0.0 collective-permute-done.2.above
  20.2 0.0 collective-permute-done.3.below
  20.2 0.8 %outer.1 = bf16[48,16,128]{2,1,0:T(8,128)(2,1)S(1)} custom-call(bf16[16,24,128]{2,1,0:T(8,128)(2,1)S(1)} %get-tuple-element.20.own, bf16[18,16,128]{2,1,0:T(8,128)(2,1)S(1)} %collective-permute-done.up, bf16[18,16,128]{2,1,0:T(8,128)(2,1)S(1)} %collective-permute-done.1.down, bf16[25,256,256]{2,1,0:T(8,128)(2,1)S(1)} %get-tuple-element.23.matrix, ...), custom_call_target="tpu_custom_call" | custom-call | tf_op jit(solution)/shard_map/outer/pallas_call | solution.py:340
  21.0 13.5 %all_to_all.10.fields = bf16[48,16,128]{2,1,0:T(8,128)(2,1)S(1)} all-to-all(bf16[48,16,128]{2,1,0:T(8,128)(2,1)S(1)} %outer.1), channel_id=1, replica_groups=mesh['freq'=16,'row'=16] {'freq'}, dimensions={0} | all-to-all | bytes 393216 | tf_op jit(solution)/shard_map/all_to_all | solution.py:494
  34.4 0.0 copy-done
  34.4 0.0 copy-done.1
  34.4 1.3 %lags.2 = f32[32,8,128]{2,1,0:T(8,128)S(1)} custom-call(s32[16]{0:T(128)S(1)} %copy-done.1, bf16[48,16,128]{2,1,0:T(8,128)(2,1)S(1)} %all_to_all.10.fields, bf16[256,2048]{1,0:T(8,128)(2,1)S(1)} %copy-done), custom_call_target="tpu_custom_call" | custom-call | tf_op jit(solution)/shard_map/lags/pallas_call | solution.py:396
  35.7 9.1 %all_to_all.11.raw = f32[32,8,128]{2,1,0:T(8,128)S(1)} all-to-all(f32[32,8,128]{2,1,0:T(8,128)S(1)} %lags.2), channel_id=1, replica_groups=mesh['freq'=16,'row'=16] {'freq'}, dimensions={0} | all-to-all | bytes 262144 | tf_op jit(solution)/shard_map/all_to_all | solution.py:496
  44.8 1.3 %image.1 = f32[2,1,16,512]{3,2,1,0:T(8,128)} custom-call(f32[81,8,128]{2,1,0:T(8,128)S(1)} %get-tuple-element.19.splats, f32[32,8,128]{2,1,0:T(8,128)S(1)} %all_to_all.11.raw), custom_call_target="tpu_custom_call" | custom-call | tf_op jit(solution)/shard_map/image/pallas_call | solution.py:458
Async XLA Ops:
  1.1 10.8 %collective-permute-start = (bf16[18,16,128]{2,1,0:T(8,128)(2,1)S(1)}, bf16[18,16,128]{2,1,0:T(8,128)(2,1)S(1)}, u32[]{:S(2)}, u32[]{:S(2)}) collective-permute-start(bf16[18,16,128]{2,1,0:T(8,128)(2,1)S(1)} %get-tuple-element.21), channel_id=1, source_target_pairs={{0,1},{1,2},{2,3},{3,4},{4,5},{5,6},{6,7},{7,8},{8,9},{9,10},{10,1... | collective-permute-start | bytes 221192 | tf_op jit(solution)/shard_map/ppermute | solution.py:477
  3.6 8.3 %collective-permute-start.1 = (bf16[18,16,128]{2,1,0:T(8,128)(2,1)S(1)}, bf16[18,16,128]{2,1,0:T(8,128)(2,1)S(1)}, u32[]{:S(2)}, u32[]{:S(2)}) collective-permute-start(bf16[18,16,128]{2,1,0:T(8,128)(2,1)S(1)} %get-tuple-element.22), channel_id=1, source_target_pairs={{0,15},{1,0},{2,1},{3,2},{4,3},{5,4},{6,5},{7,6},{8,7},{9,8},{10,9... | collective-permute-start | bytes 221192 | tf_op jit(solution)/shard_map/ppermute | solution.py:477
  13.4 6.8 %collective-permute-start.2 = (bf16[12,16,128]{2,1,0:T(8,128)(2,1)S(1)}, bf16[12,16,128]{2,1,0:T(8,128)(2,1)S(1)}, u32[]{:S(2)}, u32[]{:S(2)}) collective-permute-start(bf16[12,16,128]{2,1,0:T(8,128)(2,1)S(1)} %get-tuple-element.27), channel_id=1, source_target_pairs={{0,1},{1,2},{2,3},{3,4},{4,5},{5,6},{6,7},{7,8},{8,9},{9,10},{10,1... | collective-permute-start | bytes 147464 | tf_op jit(solution)/shard_map/ppermute | solution.py:477
  13.5 6.7 %collective-permute-start.3 = (bf16[12,16,128]{2,1,0:T(8,128)(2,1)S(1)}, bf16[12,16,128]{2,1,0:T(8,128)(2,1)S(1)}, u32[]{:S(2)}, u32[]{:S(2)}) collective-permute-start(bf16[12,16,128]{2,1,0:T(8,128)(2,1)S(1)} %get-tuple-element.28), channel_id=1, source_target_pairs={{0,15},{1,0},{2,1},{3,2},{4,3},{5,4},{6,5},{7,6},{8,7},{9,8},{10,9... | collective-permute-start | bytes 147464 | tf_op jit(solution)/shard_map/ppermute | solution.py:477
  18.7 15.7 %copy-start = (bf16[256,2048]{1,0:T(8,128)(2,1)S(1)}, bf16[256,2048]{1,0:T(8,128)(2,1)}, u32[]{:S(2)}) copy-start(bf16[256,2048]{1,0:T(8,128)(2,1)} %constant.2.clone.table) | copy-start | bytes 3145732
  18.7 15.7 %copy-start.1 = (s32[16]{0:T(128)S(1)}, s32[16]{0:T(128)}, u32[]{:S(2)}) copy-start(s32[16]{0:T(128)} %lags.3) | copy-start | bytes 196

commit v5 on v4

--- a/solution.py
+++ b/solution.py
@@ -76,15 +76,15 @@
     ]
     for copy in copies:
         copy.start()
-    for copy in copies:
-        copy.wait()
     lane = lane_ids((8, LANES))
-    planes = (
-        (source[0, 0].astype(F32), source[0, 1].astype(F32)),
-        (receiver[0, 0].astype(F32), -receiver[0, 1].astype(F32)),
-        (index[0].astype(F32), index[1].astype(F32)),
-    )
-    for p, (one, two) in enumerate(planes):
+    for p in range(3):
+        copies[p].wait()
+        if p == 0:
+            one, two = source[0, 0].astype(F32), source[0, 1].astype(F32)
+        elif p == 1:
+            one, two = receiver[0, 0].astype(F32), -receiver[0, 1].astype(F32)
+        else:
+            one, two = index[0].astype(F32), index[1].astype(F32)
         classes = []
         for group in range(ROWS // 8):
             rows = slice(8 * group, 8 * group + 8)
@@ -106,6 +106,8 @@
                 at = (ROWS + i // 2, slice(8 * (i % 2), 8 * (i % 2) + 8))
                 north[at] = classes[i].astype(BF16)
                 south[at] = classes[ROWS - OHALF + i].astype(BF16)
+    for copy in copies[3:]:
+        copy.wait()
 
 
 def in_vmem(*arrays):
@@ -322,16 +324,21 @@
     place_rows(low, HALF, jnp.where(here < last, below[...].astype(F32), 0.0))
     lines[0:EXT] = done[...]
 
-    def edge(buffer, shift, taps):
+    def edge(buffer, start, count, taps):
         acc = None
         for a in taps:
-            layer = buffer[a - shift : a - shift + HALF].reshape(HALF * 16, 2 * LANES)
+            at = start + a
+            layer = buffer[at : at + count].reshape(count * 16, 2 * LANES)
             term = jnp.dot(layer, matrix[a], preferred_element_type=F32)
             acc = term if acc is None else acc + term
-        return acc.reshape(HALF, 16, 2 * LANES)
-
-    top = part[0:HALF] + edge(high, 0, range(HALF))
-    bottom = part[HALF:EXT] + edge(low, HALF, range(HALF + 1, FILT))
+        return acc.reshape(count, 16, 2 * LANES)
+
+    few = HALF // 2
+    wide = part[0:HALF] + edge(high, 0, HALF, range(few))
+    top = jnp.concatenate([wide[:few] + edge(high, 0, few, range(few, HALF)), wide[few:]], axis=0)
+    wide = part[HALF:EXT] + edge(low, -HALF, HALF, range(HALF + 1 + few, FILT))
+    rest = edge(low, few - HALF, few, range(HALF + 1, HALF + 1 + few))
+    bottom = jnp.concatenate([wide[:few], wide[few:] + rest], axis=0)
     for x, q in enumerate(pick((top, bottom), own, up, down, 1)):
         lines[EXT + x] = q.astype(BF16)
 

time: 46.3 us -> 46.2 us (level)
  no operation moved by 1% of the time
where the time goes in v5:
time: 46.2 us; the launch traced here: 46.1 us
  blocking collectives  22.5 us (49%)
  starting transfers between devices  14.5 us (31%)
  Pallas kernels  8.39 us (18%)
  waiting for transfers between devices  0.57 us (1%)
    ppermute x4, starting transfers between devices, shifted(): lax.ppermute(x, 'row', [(i, (i + step) % count) for i in range(count)])  14.5 us
    all_to_all x1, blocking collectives, body(): fields = lax.all_to_all(lines, 'freq', 0, 0, tiled=True)  13.5 us
    all_to_all x1, blocking collectives, body(): raw = lax.all_to_all(raw, 'freq', 0, 0, tiled=True)  9.06 us
    pallas_call x1, Pallas kernels, first_step(): pl.pallas_call(first_kernel, out_shape=(pltpu.VMEM((EXT, 16, LANES), BF16...  1.45 us
    pallas_call x1, Pallas kernels, inner_step(): pl.pallas_call(inner_kernel, out_shape=(pltpu.VMEM((EXT, 16, 2 * LANES),...  1.44 us
    pallas_call x1, Pallas kernels, filter_image(): pl.pallas_call(image_kernel, out_shape=jax.ShapeDtypeStruct((DEPTHS, 1, R...  1.3 us
    pallas_call x1, Pallas kernels, gather_lags(): pl.pallas_call(gather_kernel, out_shape=pltpu.VMEM((2 * NOFF, NB, LANES),...  1.3 us
    pallas_call x1, Pallas kernels, prep(): pl.pallas_call(prep_kernel, out_shape=(pltpu.VMEM((ROWS, 24, LANES), BF16...  1.09 us
  transfers between devices with their start and end apart: 4, of which 1 were waited for; matrix products, arithmetic and copies ran while one was open for 0% of the time, Pallas kernels for 5%

profile of v5, /device:TPU:1, one launch (start us, length us, event | category | flops | bytes accessed | tf_op | source)
XLA Modules:
  0.0 46.1 jit_solution(4628654161661004065)
XLA Ops:
  0.0 1.1 %prep.1 = (bf16[16,24,128]{2,1,0:T(8,128)(2,1)S(1)}, bf16[18,16,128]{2,1,0:T(8,128)(2,1)S(1)}, bf16[18,16,128]{2,1,0:T(8,128)(2,1)S(1)}, bf16[1,2,25,2,25]{4,3,2,1,0:T(2,128)(2,1)S(1)}, f32[9,1,9]{2,1,0:T(1,128)S(1)}) custom-call(bf16[1,2,16,512]{3,2,1,0:T(8,128)(2,1)} %source_in.1, bf16[1,2,16,512]{3,2,1,0:T(8,128)(2,1)} %receiver_in.1, ...), custom_call_target="tpu_custom_call" | custom-call | tf_op jit(solution)/shard_map/prep/pallas_call | solution.py:128
  1.1 2.5 %collective-permute-start = (bf16[18,16,128]{2,1,0:T(8,128)(2,1)S(1)}, bf16[18,16,128]{2,1,0:T(8,128)(2,1)S(1)}, u32[]{:S(2)}, u32[]{:S(2)}) collective-permute-start(bf16[18,16,128]{2,1,0:T(8,128)(2,1)S(1)} %get-tuple-element.21), channel_id=1, source_target_pairs={{0,1},{1,2},{2,3},{3,4},{4,5},{5,6},{6,7},{7,8},{8,9},{9,10},{10,1... | collective-permute-start | bytes 221192 | tf_op jit(solution)/shard_map/ppermute | solution.py:484
  3.6 6.7 %collective-permute-start.1 = (bf16[18,16,128]{2,1,0:T(8,128)(2,1)S(1)}, bf16[18,16,128]{2,1,0:T(8,128)(2,1)S(1)}, u32[]{:S(2)}, u32[]{:S(2)}) collective-permute-start(bf16[18,16,128]{2,1,0:T(8,128)(2,1)S(1)} %get-tuple-element.22), channel_id=1, source_target_pairs={{0,15},{1,0},{2,1},{3,2},{4,3},{5,4},{6,5},{7,6},{8,7},{9,8},{10,9... | collective-permute-start | bytes 221192 | tf_op jit(solution)/shard_map/ppermute | solution.py:484
  10.3 1.1 %matrix.1 = (bf16[25,256,256]{2,1,0:T(8,128)(2,1)S(1)}, f32[81,8,128]{2,1,0:T(8,128)S(1)}) custom-call(bf16[1,2,25,2,25]{4,3,2,1,0:T(2,128)(2,1)S(1)} %get-tuple-element.17.filters, f32[9,1,9]{2,1,0:T(1,128)S(1)} %get-tuple-element.18.taps), custom_call_target="tpu_custom_call" | custom-call | tf_op jit(solution)/shard_map/matrix/pallas_call | solution.py:197
  11.4 0.6 %collective-permute-done.up = bf16[18,16,128]{2,1,0:T(8,128)(2,1)S(1)} collective-permute-done((bf16[18,16,128]{2,1,0:T(8,128)(2,1)S(1)}, bf16[18,16,128]{2,1,0:T(8,128)(2,1)S(1)}, u32[]{:S(2)}, u32[]{:S(2)}) %collective-permute-start) | collective-permute-done | bytes 73760 | tf_op jit(solution)/shard_map/ppermute | solution.py:484
  11.9 0.0 collective-permute-done.1.down
  12.0 1.4 %first.1 = (bf16[24,16,128]{2,1,0:T(8,128)(2,1)S(1)}, bf16[12,16,128]{2,1,0:T(8,128)(2,1)S(1)}, bf16[12,16,128]{2,1,0:T(8,128)(2,1)S(1)}) custom-call(bf16[16,24,128]{2,1,0:T(8,128)(2,1)S(1)} %get-tuple-element.20.own, bf16[18,16,128]{2,1,0:T(8,128)(2,1)S(1)} %collective-permute-done.up, bf16[18,16,128]{2,1,0:T(8,128)(2,1)S(1)} %collective-permute-done.1.down, ...), custom_call_target="tpu_custom_call" | custom-call | tf_op jit(solution)/shard_map/first/pallas_call | solution.py:282
  13.4 0.1 collective-permute-start.2
  13.5 5.2 %collective-permute-start.3 = (bf16[12,16,128]{2,1,0:T(8,128)(2,1)S(1)}, bf16[12,16,128]{2,1,0:T(8,128)(2,1)S(1)}, u32[]{:S(2)}, u32[]{:S(2)}) collective-permute-start(bf16[12,16,128]{2,1,0:T(8,128)(2,1)S(1)} %get-tuple-element.28), channel_id=1, source_target_pairs={{0,15},{1,0},{2,1},{3,2},{4,3},{5,4},{6,5},{7,6},{8,7},{9,8},{10,9... | collective-permute-start | bytes 147464 | tf_op jit(solution)/shard_map/ppermute | solution.py:484
  18.7 0.0 copy-start
  18.7 0.0 copy-start.1
  18.7 1.4 %inner.1 = (f32[24,16,256]{2,1,0:T(8,128)S(1)}, bf16[24,16,128]{2,1,0:T(8,128)(2,1)S(1)}) custom-call(bf16[24,16,128]{2,1,0:T(8,128)(2,1)S(1)} %get-tuple-element.24.done, bf16[25,256,256]{2,1,0:T(8,128)(2,1)S(1)} %get-tuple-element.23.matrix), custom_call_target="tpu_custom_call" | custom-call | tf_op jit(solution)/shard_map/inner/pallas_call | solution.py:303
  20.2 0.0 collective-permute-done.2.above
  20.2 0.0 collective-permute-done.3.below
  20.2 0.7 %outer.1 = bf16[48,16,128]{2,1,0:T(8,128)(2,1)S(1)} custom-call(bf16[16,24,128]{2,1,0:T(8,128)(2,1)S(1)} %get-tuple-element.20.own, bf16[18,16,128]{2,1,0:T(8,128)(2,1)S(1)} %collective-permute-done.up, bf16[18,16,128]{2,1,0:T(8,128)(2,1)S(1)} %collective-permute-done.1.down, bf16[25,256,256]{2,1,0:T(8,128)(2,1)S(1)} %get-tuple-element.23.matrix, ...), custom_call_target="tpu_custom_call" | custom-call | tf_op jit(solution)/shard_map/outer/pallas_call | solution.py:347
  20.9 13.5 %all_to_all.10.fields = bf16[48,16,128]{2,1,0:T(8,128)(2,1)S(1)} all-to-all(bf16[48,16,128]{2,1,0:T(8,128)(2,1)S(1)} %outer.1), channel_id=1, replica_groups=mesh['freq'=16,'row'=16] {'freq'}, dimensions={0} | all-to-all | bytes 393216 | tf_op jit(solution)/shard_map/all_to_all | solution.py:501
  34.4 0.0 copy-done
  34.4 0.0 copy-done.1
  34.4 1.3 %lags.2 = f32[32,8,128]{2,1,0:T(8,128)S(1)} custom-call(s32[16]{0:T(128)S(1)} %copy-done.1, bf16[48,16,128]{2,1,0:T(8,128)(2,1)S(1)} %all_to_all.10.fields, bf16[256,2048]{1,0:T(8,128)(2,1)S(1)} %copy-done), custom_call_target="tpu_custom_call" | custom-call | tf_op jit(solution)/shard_map/lags/pallas_call | solution.py:403
  35.7 9.1 %all_to_all.11.raw = f32[32,8,128]{2,1,0:T(8,128)S(1)} all-to-all(f32[32,8,128]{2,1,0:T(8,128)S(1)} %lags.2), channel_id=1, replica_groups=mesh['freq'=16,'row'=16] {'freq'}, dimensions={0} | all-to-all | bytes 262144 | tf_op jit(solution)/shard_map/all_to_all | solution.py:503
  44.8 1.3 %image.1 = f32[2,1,16,512]{3,2,1,0:T(8,128)} custom-call(f32[81,8,128]{2,1,0:T(8,128)S(1)} %get-tuple-element.19.splats, f32[32,8,128]{2,1,0:T(8,128)S(1)} %all_to_all.11.raw), custom_call_target="tpu_custom_call" | custom-call | tf_op jit(solution)/shard_map/image/pallas_call | solution.py:465
Async XLA Ops:
  1.1 10.8 %collective-permute-start = (bf16[18,16,128]{2,1,0:T(8,128)(2,1)S(1)}, bf16[18,16,128]{2,1,0:T(8,128)(2,1)S(1)}, u32[]{:S(2)}, u32[]{:S(2)}) collective-permute-start(bf16[18,16,128]{2,1,0:T(8,128)(2,1)S(1)} %get-tuple-element.21), channel_id=1, source_target_pairs={{0,1},{1,2},{2,3},{3,4},{4,5},{5,6},{6,7},{7,8},{8,9},{9,10},{10,1... | collective-permute-start | bytes 221192 | tf_op jit(solution)/shard_map/ppermute | solution.py:484
  3.6 8.3 %collective-permute-start.1 = (bf16[18,16,128]{2,1,0:T(8,128)(2,1)S(1)}, bf16[18,16,128]{2,1,0:T(8,128)(2,1)S(1)}, u32[]{:S(2)}, u32[]{:S(2)}) collective-permute-start(bf16[18,16,128]{2,1,0:T(8,128)(2,1)S(1)} %get-tuple-element.22), channel_id=1, source_target_pairs={{0,15},{1,0},{2,1},{3,2},{4,3},{5,4},{6,5},{7,6},{8,7},{9,8},{10,9... | collective-permute-start | bytes 221192 | tf_op jit(solution)/shard_map/ppermute | solution.py:484
  13.4 6.8 %collective-permute-start.2 = (bf16[12,16,128]{2,1,0:T(8,128)(2,1)S(1)}, bf16[12,16,128]{2,1,0:T(8,128)(2,1)S(1)}, u32[]{:S(2)}, u32[]{:S(2)}) collective-permute-start(bf16[12,16,128]{2,1,0:T(8,128)(2,1)S(1)} %get-tuple-element.27), channel_id=1, source_target_pairs={{0,1},{1,2},{2,3},{3,4},{4,5},{5,6},{6,7},{7,8},{8,9},{9,10},{10,1... | collective-permute-start | bytes 147464 | tf_op jit(solution)/shard_map/ppermute | solution.py:484
  13.5 6.7 %collective-permute-start.3 = (bf16[12,16,128]{2,1,0:T(8,128)(2,1)S(1)}, bf16[12,16,128]{2,1,0:T(8,128)(2,1)S(1)}, u32[]{:S(2)}, u32[]{:S(2)}) collective-permute-start(bf16[12,16,128]{2,1,0:T(8,128)(2,1)S(1)} %get-tuple-element.28), channel_id=1, source_target_pairs={{0,15},{1,0},{2,1},{3,2},{4,3},{5,4},{6,5},{7,6},{8,7},{9,8},{10,9... | collective-permute-start | bytes 147464 | tf_op jit(solution)/shard_map/ppermute | solution.py:484
  18.7 15.7 %copy-start = (bf16[256,2048]{1,0:T(8,128)(2,1)S(1)}, bf16[256,2048]{1,0:T(8,128)(2,1)}, u32[]{:S(2)}) copy-start(bf16[256,2048]{1,0:T(8,128)(2,1)} %constant.2.clone.table) | copy-start | bytes 3145732
  18.7 15.7 %copy-start.1 = (s32[16]{0:T(128)S(1)}, s32[16]{0:T(128)}, u32[]{:S(2)}) copy-start(s32[16]{0:T(128)} %lags.3) | copy-start | bytes 196

commit v6 on v5

--- a/solution.py
+++ b/solution.py
@@ -290,24 +290,20 @@
     )(*in_vmem(own, up, down, matrix))
 
 
-def inner_kernel(done, matrix, acc, lines, mid):
+def inner_kernel(done, matrix, acc, mid):
     zero = jnp.zeros((HALF, 16, 2 * LANES), BF16)
     mid[0:HALF] = zero
     mid[HALF + EXT :] = zero
     place_rows(mid, HALF, done[...].astype(F32))
     acc[...] = filter_rows(mid, matrix)
-    lines[...] = done[...]
 
 
 def inner_step(done, matrix):
     return pl.pallas_call(
         inner_kernel,
-        out_shape=(
-            pltpu.VMEM((EXT, 16, 2 * LANES), F32),
-            pltpu.VMEM((EXT, 16, LANES), BF16),
-        ),
+        out_shape=pltpu.VMEM((EXT, 16, 2 * LANES), F32),
         in_specs=[VSPEC] * 2,
-        out_specs=(VSPEC, VSPEC),
+        out_specs=VSPEC,
         scratch_shapes=[pltpu.VMEM((MID, 16, 2 * LANES), BF16)],
         compiler_params=PARAMS,
         name="inner",
@@ -496,7 +492,7 @@
     done, south, north = first_step(own, up, down, matrix)
     above = shifted(south, 1)
     below = shifted(north, -1)
-    part, done = inner_step(done, matrix)
+    part = inner_step(done, matrix)
     lines = outer_step(own, up, down, matrix, part, done, above, below)
     fields = lax.all_to_all(lines, "freq", 0, 0, tiled=True)
     raw = gather_lags(lags, fields)

time: 46.2 us -> 46.2 us (level)
  no operation moved by 1% of the time
where the time goes in v6:
time: 46.2 us; the launch traced here: 46.1 us
  blocking collectives  22.5 us (49%)
  starting transfers between devices  14.5 us (31%)
  Pallas kernels  8.37 us (18%)
  waiting for transfers between devices  0.57 us (1%)
    ppermute x4, starting transfers between devices, shifted(): lax.ppermute(x, 'row', [(i, (i + step) % count) for i in range(count)])  14.5 us
    all_to_all x1, blocking collectives, body(): fields = lax.all_to_all(lines, 'freq', 0, 0, tiled=True)  13.4 us
    all_to_all x1, blocking collectives, body(): raw = lax.all_to_all(raw, 'freq', 0, 0, tiled=True)  9.07 us
    pallas_call x1, Pallas kernels, first_step(): pl.pallas_call(first_kernel, out_shape=(pltpu.VMEM((EXT, 16, LANES), BF16...  1.44 us
    pallas_call x1, Pallas kernels, inner_step(): pl.pallas_call(inner_kernel, out_shape=pltpu.VMEM((EXT, 16, 2 * LANES), F...  1.44 us
    pallas_call x1, Pallas kernels, filter_image(): pl.pallas_call(image_kernel, out_shape=jax.ShapeDtypeStruct((DEPTHS, 1, R...  1.3 us
    pallas_call x1, Pallas kernels, gather_lags(): pl.pallas_call(gather_kernel, out_shape=pltpu.VMEM((2 * NOFF, NB, LANES),...  1.29 us
    pallas_call x1, Pallas kernels, prep(): pl.pallas_call(prep_kernel, out_shape=(pltpu.VMEM((ROWS, 24, LANES), BF16...  1.09 us
  transfers between devices with their start and end apart: 4, of which 1 were waited for; matrix products, arithmetic and copies ran while one was open for 0% of the time, Pallas kernels for 5%

profile of v6, /device:TPU:1, one launch (start us, length us, event | category | flops | bytes accessed | tf_op | source)
XLA Modules:
  0.0 46.1 jit_solution(8607784956649014973)
XLA Ops:
  0.0 1.1 %prep.1 = (bf16[16,24,128]{2,1,0:T(8,128)(2,1)S(1)}, bf16[18,16,128]{2,1,0:T(8,128)(2,1)S(1)}, bf16[18,16,128]{2,1,0:T(8,128)(2,1)S(1)}, bf16[1,2,25,2,25]{4,3,2,1,0:T(2,128)(2,1)S(1)}, f32[9,1,9]{2,1,0:T(1,128)S(1)}) custom-call(bf16[1,2,16,512]{3,2,1,0:T(8,128)(2,1)} %source_in.1, bf16[1,2,16,512]{3,2,1,0:T(8,128)(2,1)} %receiver_in.1, ...), custom_call_target="tpu_custom_call" | custom-call | tf_op jit(solution)/shard_map/prep/pallas_call | solution.py:128
  1.1 2.5 %collective-permute-start = (bf16[18,16,128]{2,1,0:T(8,128)(2,1)S(1)}, bf16[18,16,128]{2,1,0:T(8,128)(2,1)S(1)}, u32[]{:S(2)}, u32[]{:S(2)}) collective-permute-start(bf16[18,16,128]{2,1,0:T(8,128)(2,1)S(1)} %get-tuple-element.19), channel_id=1, source_target_pairs={{0,1},{1,2},{2,3},{3,4},{4,5},{5,6},{6,7},{7,8},{8,9},{9,10},{10,1... | collective-permute-start | bytes 221192 | tf_op jit(solution)/shard_map/ppermute | solution.py:480
  3.6 6.7 %collective-permute-start.1 = (bf16[18,16,128]{2,1,0:T(8,128)(2,1)S(1)}, bf16[18,16,128]{2,1,0:T(8,128)(2,1)S(1)}, u32[]{:S(2)}, u32[]{:S(2)}) collective-permute-start(bf16[18,16,128]{2,1,0:T(8,128)(2,1)S(1)} %get-tuple-element.20), channel_id=1, source_target_pairs={{0,15},{1,0},{2,1},{3,2},{4,3},{5,4},{6,5},{7,6},{8,7},{9,8},{10,9... | collective-permute-start | bytes 221192 | tf_op jit(solution)/shard_map/ppermute | solution.py:480
  10.3 1.1 %matrix.1 = (bf16[25,256,256]{2,1,0:T(8,128)(2,1)S(1)}, f32[81,8,128]{2,1,0:T(8,128)S(1)}) custom-call(bf16[1,2,25,2,25]{4,3,2,1,0:T(2,128)(2,1)S(1)} %get-tuple-element.15.filters, f32[9,1,9]{2,1,0:T(1,128)S(1)} %get-tuple-element.16.taps), custom_call_target="tpu_custom_call" | custom-call | tf_op jit(solution)/shard_map/matrix/pallas_call | solution.py:197
  11.4 0.6 %collective-permute-done.up = bf16[18,16,128]{2,1,0:T(8,128)(2,1)S(1)} collective-permute-done((bf16[18,16,128]{2,1,0:T(8,128)(2,1)S(1)}, bf16[18,16,128]{2,1,0:T(8,128)(2,1)S(1)}, u32[]{:S(2)}, u32[]{:S(2)}) %collective-permute-start) | collective-permute-done | bytes 73760 | tf_op jit(solution)/shard_map/ppermute | solution.py:480
  11.9 0.0 collective-permute-done.1.down
  12.0 1.4 %first.1 = (bf16[24,16,128]{2,1,0:T(8,128)(2,1)S(1)}, bf16[12,16,128]{2,1,0:T(8,128)(2,1)S(1)}, bf16[12,16,128]{2,1,0:T(8,128)(2,1)S(1)}) custom-call(bf16[16,24,128]{2,1,0:T(8,128)(2,1)S(1)} %get-tuple-element.18.own, bf16[18,16,128]{2,1,0:T(8,128)(2,1)S(1)} %collective-permute-done.up, bf16[18,16,128]{2,1,0:T(8,128)(2,1)S(1)} %collective-permute-done.1.down, ...), custom_call_target="tpu_custom_call" | custom-call | tf_op jit(solution)/shard_map/first/pallas_call | solution.py:282
  13.4 0.1 collective-permute-start.2
  13.5 5.2 %collective-permute-start.3 = (bf16[12,16,128]{2,1,0:T(8,128)(2,1)S(1)}, bf16[12,16,128]{2,1,0:T(8,128)(2,1)S(1)}, u32[]{:S(2)}, u32[]{:S(2)}) collective-permute-start(bf16[12,16,128]{2,1,0:T(8,128)(2,1)S(1)} %get-tuple-element.24), channel_id=1, source_target_pairs={{0,15},{1,0},{2,1},{3,2},{4,3},{5,4},{6,5},{7,6},{8,7},{9,8},{10,9... | collective-permute-start | bytes 147464 | tf_op jit(solution)/shard_map/ppermute | solution.py:480
  18.7 1.4 %inner.1.part = f32[24,16,256]{2,1,0:T(8,128)S(1)} custom-call(bf16[24,16,128]{2,1,0:T(8,128)(2,1)S(1)} %get-tuple-element.22.done, bf16[25,256,256]{2,1,0:T(8,128)(2,1)S(1)} %get-tuple-element.21.matrix), custom_call_target="tpu_custom_call" | custom-call | tf_op jit(solution)/shard_map/inner/pallas_call | solution.py:302
  20.2 0.0 copy-start
  20.2 0.0 copy-start.1
  20.2 0.0 collective-permute-done.2.above
  20.2 0.0 collective-permute-done.3.below
  20.2 0.7 %outer.1 = bf16[48,16,128]{2,1,0:T(8,128)(2,1)S(1)} custom-call(bf16[16,24,128]{2,1,0:T(8,128)(2,1)S(1)} %get-tuple-element.18.own, bf16[18,16,128]{2,1,0:T(8,128)(2,1)S(1)} %collective-permute-done.up, bf16[18,16,128]{2,1,0:T(8,128)(2,1)S(1)} %collective-permute-done.1.down, bf16[25,256,256]{2,1,0:T(8,128)(2,1)S(1)} %get-tuple-element.21.matrix, ...), custom_call_target="tpu_custom_call" | custom-call | tf_op jit(solution)/shard_map/outer/pallas_call | solution.py:343
  20.9 13.4 %all_to_all.10.fields = bf16[48,16,128]{2,1,0:T(8,128)(2,1)S(1)} all-to-all(bf16[48,16,128]{2,1,0:T(8,128)(2,1)S(1)} %outer.1), channel_id=1, replica_groups=mesh['freq'=16,'row'=16] {'freq'}, dimensions={0} | all-to-all | bytes 393216 | tf_op jit(solution)/shard_map/all_to_all | solution.py:497
  34.4 0.0 copy-done
  34.4 0.0 copy-done.1
  34.4 1.3 %lags.2 = f32[32,8,128]{2,1,0:T(8,128)S(1)} custom-call(s32[16]{0:T(128)S(1)} %copy-done.1, bf16[48,16,128]{2,1,0:T(8,128)(2,1)S(1)} %all_to_all.10.fields, bf16[256,2048]{1,0:T(8,128)(2,1)S(1)} %copy-done), custom_call_target="tpu_custom_call" | custom-call | tf_op jit(solution)/shard_map/lags/pallas_call | solution.py:399
  35.7 9.1 %all_to_all.11.raw = f32[32,8,128]{2,1,0:T(8,128)S(1)} all-to-all(f32[32,8,128]{2,1,0:T(8,128)S(1)} %lags.2), channel_id=1, replica_groups=mesh['freq'=16,'row'=16] {'freq'}, dimensions={0} | all-to-all | bytes 262144 | tf_op jit(solution)/shard_map/all_to_all | solution.py:499
  44.8 1.3 %image.1 = f32[2,1,16,512]{3,2,1,0:T(8,128)} custom-call(f32[81,8,128]{2,1,0:T(8,128)S(1)} %get-tuple-element.17.splats, f32[32,8,128]{2,1,0:T(8,128)S(1)} %all_to_all.11.raw), custom_call_target="tpu_custom_call" | custom-call | tf_op jit(solution)/shard_map/image/pallas_call | solution.py:461
Async XLA Ops:
  1.1 10.8 %collective-permute-start = (bf16[18,16,128]{2,1,0:T(8,128)(2,1)S(1)}, bf16[18,16,128]{2,1,0:T(8,128)(2,1)S(1)}, u32[]{:S(2)}, u32[]{:S(2)}) collective-permute-start(bf16[18,16,128]{2,1,0:T(8,128)(2,1)S(1)} %get-tuple-element.19), channel_id=1, source_target_pairs={{0,1},{1,2},{2,3},{3,4},{4,5},{5,6},{6,7},{7,8},{8,9},{9,10},{10,1... | collective-permute-start | bytes 221192 | tf_op jit(solution)/shard_map/ppermute | solution.py:480
  3.6 8.3 %collective-permute-start.1 = (bf16[18,16,128]{2,1,0:T(8,128)(2,1)S(1)}, bf16[18,16,128]{2,1,0:T(8,128)(2,1)S(1)}, u32[]{:S(2)}, u32[]{:S(2)}) collective-permute-start(bf16[18,16,128]{2,1,0:T(8,128)(2,1)S(1)} %get-tuple-element.20), channel_id=1, source_target_pairs={{0,15},{1,0},{2,1},{3,2},{4,3},{5,4},{6,5},{7,6},{8,7},{9,8},{10,9... | collective-permute-start | bytes 221192 | tf_op jit(solution)/shard_map/ppermute | solution.py:480
  13.4 6.8 %collective-permute-start.2 = (bf16[12,16,128]{2,1,0:T(8,128)(2,1)S(1)}, bf16[12,16,128]{2,1,0:T(8,128)(2,1)S(1)}, u32[]{:S(2)}, u32[]{:S(2)}) collective-permute-start(bf16[12,16,128]{2,1,0:T(8,128)(2,1)S(1)} %get-tuple-element.23), channel_id=1, source_target_pairs={{0,1},{1,2},{2,3},{3,4},{4,5},{5,6},{6,7},{7,8},{8,9},{9,10},{10,1... | collective-permute-start | bytes 147464 | tf_op jit(solution)/shard_map/ppermute | solution.py:480
  13.5 6.7 %collective-permute-start.3 = (bf16[12,16,128]{2,1,0:T(8,128)(2,1)S(1)}, bf16[12,16,128]{2,1,0:T(8,128)(2,1)S(1)}, u32[]{:S(2)}, u32[]{:S(2)}) collective-permute-start(bf16[12,16,128]{2,1,0:T(8,128)(2,1)S(1)} %get-tuple-element.24), channel_id=1, source_target_pairs={{0,15},{1,0},{2,1},{3,2},{4,3},{5,4},{6,5},{7,6},{8,7},{9,8},{10,9... | collective-permute-start | bytes 147464 | tf_op jit(solution)/shard_map/ppermute | solution.py:480
  20.2 14.2 %copy-start = (bf16[256,2048]{1,0:T(8,128)(2,1)S(1)}, bf16[256,2048]{1,0:T(8,128)(2,1)}, u32[]{:S(2)}) copy-start(bf16[256,2048]{1,0:T(8,128)(2,1)} %constant.2.clone.table) | copy-start | bytes 3145732
  20.2 14.2 %copy-start.1 = (s32[16]{0:T(128)S(1)}, s32[16]{0:T(128)}, u32[]{:S(2)}) copy-start(s32[16]{0:T(128)} %lags.3) | copy-start | bytes 196
